TPU v7x, 128 devices: a whole 4x4x4 slice. The times are simulated.
128 devices in a mesh: role: 4 (over x_hi, core), brick: 32 (over y, x_lo, z).
Axes of the slice: x: 4 (x_hi: 2, x_lo: 2; x = x_hi * 2 + x_lo), y: 4, z: 4, core: 2. Of those that a mesh axis runs over, the one named last changes fastest.
Arguments:
- velocity: float32 [3, 64, 512, 128], P(None, 'role', 'brick'), may hold values from -6 to 6
- first_layer: float32 [1536, 1024], P('brick'), may hold values from -0.15625 to 0.15625
- middle_layer: float32 [1024, 1024], P('brick'), may hold values from -0.1875 to 0.1875
- last_layer: float32 [1536, 1024], P('brick'), may hold values from -0.1875 to 0.1875
- first_moment: float32 [1536, 1024], P('brick'), may hold values from -0.06 to 0.06
- middle_moment: float32 [1024, 1024], P('brick'), may hold values from -0.06 to 0.06
- last_moment: float32 [1536, 1024], P('brick'), may hold values from -0.06 to 0.06
- patch_pick: int32 [16384], P(('role', 'brick')), may hold values from 0 to 63
- target_rows: bfloat16 [16384, 1536], P(('role', 'brick')), may hold values from -6 to 6
Outputs:
- velocity_next: float32 [3, 64, 512, 128], P(None, 'role', 'brick')
- first_updated: float32 [1536, 1024], P('brick', 'role')
- middle_updated: float32 [1024, 1024], P('brick', 'role')
- last_updated: float32 [1536, 1024], P('brick', 'role')
- first_momentum: float32 [1536, 1024], P('brick', 'role')
- middle_momentum: float32 [1024, 1024], P('brick', 'role')
- last_momentum: float32 [1536, 1024], P('brick', 'role')
Inputs may be any that keep to these rules, and one draw needn't show every extreme that they name: `patch_pick`: entry q names a cube of the brick of device q // 128 in the order of patches.
All inputs are finite; a program needn't handle non-finite values. Where the computation divides by a largest or mean magnitude, that divisor is 1e-20 or more.
Results may differ from a plain program's by a relative error of at most 0.019.
Values may be sent and summed in bfloat16 or wider, within the bound.
No kernel may reach another device: no remote copies, remote signals or barrier semaphores. Data moves between devices by JAX's collectives and lax.ppermute only.
A program may use at most 128 MiB of HBM per device.

v0:
```python
import math

import jax
import jax.numpy as jnp
from jax import lax
from jax.experimental import pallas as pl
from jax.experimental.pallas import tpu as pltpu
from jax.sharding import Mesh
from jax.sharding import PartitionSpec as P


AXES = ("role_0", "role_1", "brick_0", "brick_1", "brick_2")
SIZES = (2, 2, 4, 2, 4)
ROLE = ("role_0", "role_1")
BRICK = ("brick_0", "brick_1", "brick_2")
ROWS = (48, 32, 48)
STARTS = (0, 48, 80)
BLOCK = 128
LANES = 256


weno_eps = 1e-06
courant = 0.3
momentum_keep = 0.9
learn_rate = 0.3
bf16 = jnp.bfloat16
f32 = jnp.float32


def flat_id(x, y, z, c):
    return (((x // 2) * 2 + c) * 4 + y) * 8 + (x % 2) * 4 + z


def phase_pairs(phase, shift):
    pairs = []
    for c in range(2):
        dim = (0, 1, 2)[phase] if c == 0 else (2, 0, 1)[phase]
        for x in range(4):
            for y in range(4):
                for z in range(4):
                    to = [x, y, z]
                    to[dim] = (to[dim] + shift) % 4
                    pairs.append((flat_id(x, y, z, c), flat_id(*to, c)))
    return pairs


def planes():
    ring = range(4)
    groups = [[flat_id(x, y, z, 0) for y in ring for x in ring] for z in ring]
    return groups + [[flat_id(x, y, z, 1) for x in ring for z in ring] for y in ring]


def exchange_planes(blocks):
    return lax.all_to_all(blocks, AXES, 0, 0, tiled=True, axis_index_groups=planes())


def spread(parts, phase):
    take = (lambda s: parts[s]) if isinstance(parts, (list, tuple)) else (lambda s: parts)
    return [lax.ppermute(take(s), AXES, phase_pairs(phase, s)) for s in (1, 3, 2)]


def swap_cores(array):
    return lax.ppermute(array, "role_1", [(0, 1), (1, 0)])


def places():
    core = lax.axis_index("role_1")
    x = lax.axis_index("role_0") * 2 + lax.axis_index("brick_1")
    y = lax.axis_index("brick_0")
    z = lax.axis_index("brick_2")
    first = jnp.where(core == 0, x, z)
    second = jnp.where(core == 0, y, x)
    third = jnp.where(core == 0, z, y)
    role = lax.axis_index(ROLE)
    return jnp.stack([core, first, second, third, role]).astype(jnp.int32)


VMEM = pl.BlockSpec(memory_space=pltpu.VMEM)
SMEM = pl.BlockSpec(memory_space=pltpu.SMEM)


def held(array):
    return math.prod(array.shape) * jnp.dtype(array.dtype).itemsize


def call(kernel, outs, place, *arrays, scratch=(), spare=4):
    room = sum(map(held, arrays)) + sum(map(held, jax.tree.leaves(outs))) + sum(map(held, scratch))
    return pl.pallas_call(
        kernel,
        out_shape=outs,
        in_specs=[SMEM] + [VMEM] * len(arrays),
        out_specs=jax.tree.map(lambda _: VMEM, outs),
        scratch_shapes=scratch,
        compiler_params=pltpu.CompilerParams(vmem_limit_bytes=room + (spare << 20)),
    )(place, *arrays)


def like(shape, dtype):
    return jax.ShapeDtypeStruct(shape, dtype)


def own_block_kernel(place, first, middle, last, out):
    cols = pl.ds(pl.multiple_of(place[4] * LANES, LANES), LANES)
    for ref, start, rows in zip((first, middle, last), STARTS, ROWS):
        part = ref[:, cols].astype(bf16)
        for copy in range(16):
            out[copy, start : start + rows, :] = part


def finish_kernel(place, own, one, three, two, first, middle, last):
    core, mine = place[0], place[3]
    for s, ref in ((0, own), (1, one), (3, three), (2, two)):
        at3 = lax.rem(mine + 4 - s, 4)
        for at2 in range(4):
            for at1 in range(4):
                x = jnp.where(core == 0, at1, at2)
                y = jnp.where(core == 0, at2, at3)
                z = jnp.where(core == 0, at3, at1)
                high = x // 2
                brick = y * 8 + (x - high * 2) * 4 + z
                for out, start, rows in zip((first, middle, last), STARTS, ROWS):
                    to = pl.ds(pl.multiple_of(brick * rows, 16), rows)
                    out[high, to, :] = ref[at2 * 4 + at1, start : start + rows, :]


def gather_matrices(square, place):
    got = spread(square, 2)
    mine = call(finish_kernel, tuple(like((2, 32 * rows, LANES), bf16) for rows in ROWS), place, square, *got)
    return mine, tuple(swap_cores(m) for m in mine)


def swap_blocks(tile):
    row = lax.broadcasted_iota(jnp.int32, (16, 128), 0)
    group = lax.broadcasted_iota(jnp.int32, (16, 128), 1) // 8
    for bit in (1, 2, 4, 8):
        row_set = (row & bit) != 0
        group_set = (group & bit) != 0
        down = pltpu.roll(pltpu.roll(tile, 16 - bit, 0), 8 * bit, 1)
        up = pltpu.roll(pltpu.roll(tile, bit, 0), 128 - 8 * bit, 1)
        moved = jnp.where(row_set, up, down)
        tile = jnp.where(row_set == group_set, tile, moved)
    return tile


def cut_kernel(place, field, pick, out, chosen):
    for i in range(2):
        for j in range(2):
            for g in range(12):
                c, at = g // 4, i * 8 + (g % 4) * 2
                low = field[c, at, j * 8 : j * 8 + 8, :]
                high = field[c, at + 1, j * 8 : j * 8 + 8, :]
                tile = swap_blocks(jnp.concatenate([low, high], axis=0))
                row = (i * 2 + j) * 16
                out[row : row + 16, g * 128 : g * 128 + 128] = tile.astype(bf16)
    which = lax.broadcasted_iota(jnp.int32, (BLOCK, 64), 1) == pick[...]
    chosen[...] = dot(which.astype(f32).astype(bf16), out[...]).astype(bf16)


def top_kernel(place, field, out):
    def take(n, top):
        return jnp.maximum(top, jnp.max(jnp.abs(field[n // 16, n % 16]).reshape(2, 8, 128), axis=0))

    out[...] = lax.fori_loop(0, 48, take, jnp.zeros((8, 128), f32))


def dot(a, b):
    return jnp.dot(a, b, preferred_element_type=f32)


def dot_rows(a, b):
    return lax.dot_general(a, b, (((1,), (1,)), ((), ())), preferred_element_type=f32)


def logistic(v):
    return 1.0 / (1.0 + jnp.exp(-v))


def forward_kernel(
    place, picked, targets, m1, m2, m3, o1, o2, o3, hold, share, act, slope_one, slope_two, act_two
):
    core = place[0]
    total = 128 * 128
    cells = [(half, high) for half in range(2) for high in range(2)]
    first, middle, last = (m1, o1), (m2, o2), (m3, o3)

    def role_of(half, high):
        return high * 2 + (core if half == 0 else 1 - core)

    chosen = picked[...]
    for half, high in cells:
        pre = dot(chosen, first[half][high])
        s = logistic(pre)
        r = role_of(half, high)
        act[r] = (pre * s).astype(bf16)
        slope_one[r] = s * (1.0 + pre * (1.0 - s))
    act_one = jnp.concatenate([act[r] for r in range(4)], axis=1)
    y = jnp.zeros((BLOCK, 1536), f32)
    for n, (half, high) in enumerate(cells):
        pre = dot(act_one, middle[half][high])
        s = logistic(pre)
        a = (pre * s).astype(bf16)
        act_two[n] = a
        slope_two[n] = s * (1.0 + pre * (1.0 - s))
        y = y + dot_rows(a, last[half][high])
    error = ((y - targets[...].astype(f32)) / total).astype(bf16)
    for out in (hold, share):
        out[:, 0:1536] = error
        out[:, 1536:2560] = act_one
    back_one = jnp.zeros((BLOCK, 1024), f32)
    for n, (half, high) in enumerate(cells):
        d = (dot(error, last[half][high]) * slope_two[n]).astype(bf16)
        out = share if half else hold
        out[:, 2560 + high * LANES : 2816 + high * LANES] = act_two[n]
        out[:, 3072 + high * LANES : 3328 + high * LANES] = d
        back_one = back_one + dot_rows(d, middle[half][high])
    for r in range(4):
        act[r] = (back_one[:, r * LANES : (r + 1) * LANES] * slope_one[r]).astype(bf16)
    for half, high in cells:
        out = share if half else hold
        out[:, 3584 + high * LANES : 3840 + high * LANES] = act[role_of(half, high)]


def gradient_kernel(
    place, hold, other, picked, picked_other, own, one, two, three, left_first, left_middle, left_last
):
    core, mine = place[0], place[3]

    def both(start, size):
        cols = slice(start, start + size)
        return jnp.concatenate([hold[:, cols], other[:, cols]], axis=0)

    def turned(v):
        return v.astype(f32).T.astype(bf16)

    jobs = (
        (2, left_last, both(0, 1536), 2560),
        (1, left_middle, both(1536, 1024), 3072),
        (0, left_first, jnp.concatenate([picked[...], picked_other[...]], axis=0), 3584),
    )
    for m, left, value, start in jobs:
        rows = ROWS[m]
        left[...] = turned(value).reshape(32, rows, LANES)
        for high in range(2):
            right = both(start + high * LANES, LANES)
            for s, out in enumerate((own, one, two, three)):
                at3 = lax.rem(mine + s, 4)
                parts, places_ = [], []
                for low in range(2):
                    for w in range(4):
                        x = high * 2 + low
                        brick = jnp.where(core == 0, w * 8 + at3, at3 * 8 + w) + low * 4
                        parts.append(left[brick])
                        places_.append(jnp.where(core == 0, w * 4 + x, x * 4 + w))
                grad = dot(jnp.concatenate(parts, axis=0), right).astype(bf16)
                for n, at in enumerate(places_):
                    out[at, STARTS[m] : STARTS[m] + rows, :] = grad[n * rows : (n + 1) * rows, :]


def closure_kernel(place, patches, field, m1, m2, m3, o1, o2, o3, out, act):
    core = place[0]
    cells = [(half, high) for half in range(2) for high in range(2)]
    first, middle, last = (m1, o1), (m2, o2), (m3, o3)
    rows = patches[...]
    for half, high in cells:
        pre = dot(rows, first[half][high])
        act[high * 2 + (core if half == 0 else 1 - core)] = (pre * logistic(pre)).astype(bf16)
    act_one = jnp.concatenate([act[r] for r in range(4)], axis=1)
    fix = jnp.zeros((64, 1536), f32)
    for half, high in cells:
        pre = dot(act_one, middle[half][high])
        fix = fix + dot_rows((pre * logistic(pre)).astype(bf16), last[half][high])
    fix = fix.astype(bf16).astype(f32)
    for i in range(2):
        for j in range(2):
            for g in range(12):
                row = (i * 2 + j) * 16
                tile = swap_blocks(fix[row : row + 16, g * 128 : g * 128 + 128])
                c, at = g // 4, i * 8 + (g % 4) * 2
                for a in range(2):
                    part = tile[a * 8 : a * 8 + 8, :]
                    here = (c, at + a, slice(j * 8, j * 8 + 8))
                    out[here] = field[here] + part


def total_of(refs, at):
    return sum(ref[at].astype(f32) for ref in refs)


def third_kernel(place, a, b, c, d, out):
    out[...] = total_of((a, b, c, d), slice(None)).astype(bf16)


def update_kernel(place, pieces, *refs):
    layers, moments, updated, momenta, fresh = refs[:3], refs[3:6], refs[6:9], refs[9:12], refs[12]
    cols = pl.ds(pl.multiple_of(place[4] * LANES, LANES), LANES)
    for m, (start, rows) in enumerate(zip(STARTS, ROWS)):
        grad = sum(pieces[n, start : start + rows, :].astype(f32) for n in range(16))
        momentum = momentum_keep * moments[m][:, cols] + grad
        new = layers[m][:, cols] - learn_rate * momentum
        momenta[m][...] = momentum
        updated[m][...] = new
        for copy in range(16):
            fresh[copy, start : start + rows, :] = new.astype(bf16)


def sum_plane(parts, place):
    got = spread(parts, 2)
    blocks = call(third_kernel, like((16, BLOCK, LANES), bf16), place, parts[0], *got)
    return exchange_planes(blocks)


def edges_of(field):
    rounded, found = field.astype(bf16), []
    for axis, dim in ((ROLE, 1), (BRICK, 2)):
        size, length = lax.axis_size(axis), field.shape[dim]
        up = [(i, (i + 1) % size) for i in range(size)]
        last = lax.slice_in_dim(rounded, length - 3, length, axis=dim)
        leading = lax.slice_in_dim(rounded, 0, 3, axis=dim)
        found.append(lax.ppermute(last, axis, up).astype(f32))
        found.append(lax.ppermute(leading, axis, [(b, a) for a, b in up]).astype(f32))
    return found


def blended(a, b, c, d, e):
    bend, tilt, floor = 13.0 / 12.0 / 64.0, 0.25 / 64.0, weno_eps / 64.0
    b0, b1, b2 = a - 2.0 * b + c, b - 2.0 * c + d, c - 2.0 * d + e
    t0, t1, t2 = a - 4.0 * b + 3.0 * c, b - d, 3.0 * c - 4.0 * d + e
    r0 = floor + bend * b0 * b0 + tilt * t0 * t0
    r1 = floor + bend * b1 * b1 + tilt * t1 * t1
    r2 = floor + bend * b2 * b2 + tilt * t2 * t2
    s0, s1, s2 = r0 * r0, r1 * r1, r2 * r2
    w0, w1, w2 = 0.1 * (s1 * s2), 0.6 * (s0 * s2), 0.3 * (s0 * s1)
    upper = w0 * (2.0 * a - 7.0 * b + 11.0 * c) + w1 * (5.0 * c + 2.0 * d - b) + w2 * (2.0 * c + 5.0 * d - e)
    return upper / (6.0 * (w0 + w1 + w2))


def face(plus, minus):
    return blended(*plus[0:5]) + blended(*minus[5:0:-1])


def advect_kernel(tops, field, low_x, high_x, low_y, high_y, out, top, plus_x, minus_x, rows, plus_y, minus_y, faces):
    speed = jnp.max(tops[...])

    def split(along, value):
        return 0.5 * (along * value + speed * value), 0.5 * (along * value - speed * value)

    def lay(at, planes):
        for c in range(3):
            plus_x[c, at], minus_x[c, at] = split(planes[0], planes[c])

    for n in range(3):
        lay(n, [low_x[c, n] for c in range(3)])
        lay(n + 19, [high_x[c, n] for c in range(3)])

    def inner(n, carry):
        lay(n + 3, [field[c, n] for c in range(3)])
        return carry

    lax.fori_loop(0, 16, inner, 0)
    factor = courant / speed
    top[...] = jnp.zeros((8, 128), f32)

    def face_x(c, n):
        return face([plus_x[c, n + k] for k in range(6)], [minus_x[c, n + k] for k in range(6)])

    def step(n, below):
        above = tuple(face_x(c, n + 1) for c in range(3))
        values = [field[c, n] for c in range(3)]
        for c in range(3):
            rows[c, 0:3, :] = low_y[c, n]
            rows[c, 3:19, :] = values[c]
            rows[c, 19:22, :] = high_y[c, n]
        for c in range(3):
            plus_y[...], minus_y[...] = split(rows[1], rows[c])
            faces[...] = face(
                [plus_y[k : k + 24, :] for k in range(6)], [minus_y[k : k + 24, :] for k in range(6)]
            )
            along_y = faces[1:17, :] - faces[0:16, :]
            plus, minus = split(values[2], values[c])
            shifts = (2, 1, 0, 127, 126, 125)
            edge = face(
                [pltpu.roll(plus, k, 1) if k else plus for k in shifts],
                [pltpu.roll(minus, k, 1) if k else minus for k in shifts],
            )
            along_z = edge - pltpu.roll(edge, 1, 1)
            new = values[c] - factor * ((above[c] - below[c]) + along_y + along_z)
            out[c, n] = new
            size = jnp.abs(new)
            top[...] = jnp.maximum(top[...], jnp.maximum(size[0:8, :], size[8:16, :]))
        return above

    lax.fori_loop(0, 16, step, tuple(face_x(c, 0) for c in range(3)))


def advect(tops, field, edges):
    planes, line = (3, 22, 16, 128), (32, 128)
    scratch = [pltpu.VMEM(planes, f32)] * 2 + [pltpu.VMEM((3, *line), f32)]
    scratch += [pltpu.VMEM(line, f32)] * 2 + [pltpu.VMEM((24, 128), f32)]
    return pl.pallas_call(
        advect_kernel,
        out_shape=(like(field.shape, f32), like((8, 128), f32)),
        in_specs=[VMEM] * 6,
        out_specs=(VMEM, VMEM),
        scratch_shapes=scratch,
        compiler_params=pltpu.CompilerParams(vmem_limit_bytes=8 << 20),
    )(tops, field, *edges)


def global_tops(top):
    other = swap_cores(top)
    top = jnp.maximum(top, other)
    for phase in range(3):
        others = spread(top, phase)
        for other in others:
            top = jnp.maximum(top, other)
    return top


def after(value, first):
    return lax.optimization_barrier((value, first))[0]


def one_step(current, top, first):
    tops = after(global_tops(top), first)
    edges = edges_of(current)
    return advect(tops, current, edges)


def whole(velocity, first, middle, last, first_moment, middle_moment, last_moment, patch_pick, targets):
    place = places()
    layers, moments = (first, middle, last), (first_moment, middle_moment, last_moment)
    copies = call(own_block_kernel, like((16, BLOCK, LANES), bf16), place, *layers)
    square = exchange_planes(copies)
    mine, other = gather_matrices(square, place)
    top = call(top_kernel, like((8, 128), f32), place, velocity)
    patches, chosen = call(
        cut_kernel, (like((64, 1536), bf16), like((BLOCK, 1536), bf16)), place, velocity, patch_pick.reshape(BLOCK, 1)
    )
    chosen_other = swap_cores(chosen)
    between, top = one_step(velocity, top, mine[0])
    hold, share = call(
        forward_kernel,
        (like((BLOCK, 4096), bf16),) * 2,
        place,
        chosen,
        targets,
        *mine,
        *other,
        scratch=[
            pltpu.VMEM((4, BLOCK, LANES), bf16),
            pltpu.VMEM((4, BLOCK, LANES), f32),
            pltpu.VMEM((4, BLOCK, LANES), f32),
            pltpu.VMEM((4, BLOCK, LANES), bf16),
        ],
    )
    parts = call(
        gradient_kernel,
        (like((16, BLOCK, LANES), bf16),) * 4,
        place,
        hold,
        swap_cores(share),
        chosen,
        chosen_other,
        scratch=[pltpu.VMEM((32, rows, LANES), bf16) for rows in ROWS],
    )
    between, top = lax.optimization_barrier((between, top, parts[3]))[:2]
    pieces = sum_plane(parts, place)
    wide = tuple(like((rows, LANES), f32) for rows in ROWS)
    results = call(update_kernel, wide + wide + (like((16, BLOCK, LANES), bf16),), place, pieces, *layers, *moments)
    mine, other = gather_matrices(exchange_planes(results[6]), place)
    current, _ = one_step(between, top, results[6])
    velocity_next = call(
        closure_kernel,
        like(velocity.shape, f32),
        place,
        patches,
        current,
        *mine,
        *other,
        scratch=[pltpu.VMEM((4, 64, LANES), bf16)],
    )
    return (velocity_next, *results[:6])


def solution(mesh):
    torus = Mesh(mesh.devices.reshape(SIZES), AXES)
    in_specs = (P(None, ROLE, BRICK, None),) + (P(BRICK, None),) * 6 + (P(AXES), P(AXES, None))
    out_specs = (P(None, ROLE, BRICK, None),) + (P(BRICK, ROLE),) * 6
    return jax.shard_map(whole, mesh=torus, in_specs=in_specs, out_specs=out_specs, check_vma=False)
```

profile of v0, /device:TPU:0, one launch (start us, length us, event | category | flops | bytes accessed | tf_op | source)
XLA Modules:
  0.0 253.6 jit_solution(8472266035347047884)
XLA Ops:
  4.1 25.3 %all_to_all.15.own = bf16[16,128,256]{2,1,0:T(8,128)(2,1)S(1)} all-to-all(bf16[16,128,256]{2,1,0:T(8,128)(2,1)S(1)} %shard_map.146), channel_id=1, replica_groups={{0,4,64,68,8,12,72,76,16,20,80,84,24,28,88,92},{1,5,65,69,9,13,73,77,17..., dimensions={0} | all-to-all | bytes 2097152 | tf_op jit(solution)/shard_map/all_to_all | solution.py:54
  29.4 1.5 collective-permute-start.10
  30.9 1.8 collective-permute-start.11
  32.7 1.7 collective-permute-start.12
  34.4 11.1 %collective-permute-done.10.one = bf16[16,128,256]{2,1,0:T(8,128)(2,1)S(1)} collective-permute-done((bf16[16,128,256]{2,1,0:T(8,128)(2,1)S(1)}, bf16[16,128,256]{2,1,0:T(8,128)(2,1)S(1)}, u32[]{:S(2)}, u32[]{:S(2)}) %collective-permute-start.10) | collective-permute-done | bytes 1048608 | tf_op jit(solution)/shard_map/ppermute | solution.py:59
  45.4 10.8 %collective-permute-done.11.three = bf16[16,128,256]{2,1,0:T(8,128)(2,1)S(1)} collective-permute-done((bf16[16,128,256]{2,1,0:T(8,128)(2,1)S(1)}, bf16[16,128,256]{2,1,0:T(8,128)(2,1)S(1)}, u32[]{:S(2)}, u32[]{:S(2)}) %collective-permute-start.11) | collective-permute-done | bytes 1048608 | tf_op jit(solution)/shard_map/ppermute | solution.py:59
  57.5 2.0 shard_map.147
  61.7 2.1 shard_map.144
  63.8 3.0 %collective-permute-done.18.o2 = bf16[2,1024,256]{2,1,0:T(8,128)(2,1)} collective-permute-done((bf16[2,1024,256]{2,1,0:T(8,128)(2,1)}, bf16[2,1024,256]{2,1,0:T(8,128)(2,1)}, u32[]{:S(2)}, u32[]{:S(2)}) %collective-permute-start.18) | collective-permute-done | bytes 1048608 | tf_op jit(solution)/shard_map/ppermute | solution.py:63
  67.8 6.5 %shard_map.149 = (bf16[128,4096]{1,0:T(8,128)(2,1)S(1)}, bf16[128,4096]{1,0:T(8,128)(2,1)S(1)}) custom-call(s32[5]{0:T(128)S(1)} %stack.23.place, bf16[128,1536]{1,0:T(8,128)(2,1)S(1)} %get-tuple-element.40.picked, bf16[128,1536]{1,0:T(8,128)(2,1)S(1)} %copy-done.7, bf16[2,1536,256]{2,1,0:T(8,128)(2,1)S(1)} %get-tuple-element.36.m1, ...), custom_call_target="tpu_custom_call" | custom-call | tf_op jit(solution)/shard_map/pallas_call | solution.py:88
  74.9 2.7 %collective-permute-done.21.picked_other = bf16[128,1536]{1,0:T(8,128)(2,1)S(1)} collective-permute-done((bf16[128,1536]{1,0:T(8,128)(2,1)S(1)}, bf16[128,1536]{1,0:T(8,128)(2,1)S(1)}, u32[]{:S(2)}, u32[]{:S(2)}) %collective-permute-start.21) | collective-permute-done | bytes 393248 | tf_op jit(solution)/shard_map/ppermute | solution.py:63
  77.6 2.1 shard_map.150
  79.7 1.5 collective-permute-start.32
  81.2 1.8 collective-permute-start.33
  83.7 12.1 %collective-permute-done.32.b = bf16[16,128,256]{2,1,0:T(8,128)(2,1)S(1)} collective-permute-done((bf16[16,128,256]{2,1,0:T(8,128)(2,1)S(1)}, bf16[16,128,256]{2,1,0:T(8,128)(2,1)S(1)}, u32[]{:S(2)}, u32[]{:S(2)}) %collective-permute-start.32) | collective-permute-done | bytes 1048608 | tf_op jit(solution)/shard_map/ppermute | solution.py:59
  95.8 10.8 %collective-permute-done.33.c = bf16[16,128,256]{2,1,0:T(8,128)(2,1)S(1)} collective-permute-done((bf16[16,128,256]{2,1,0:T(8,128)(2,1)S(1)}, bf16[16,128,256]{2,1,0:T(8,128)(2,1)S(1)}, u32[]{:S(2)}, u32[]{:S(2)}) %collective-permute-start.33) | collective-permute-done | bytes 1048608 | tf_op jit(solution)/shard_map/ppermute | solution.py:59
  108.8 19.7 %all_to_all.16.pieces = bf16[16,128,256]{2,1,0:T(8,128)(2,1)S(1)} all-to-all(bf16[16,128,256]{2,1,0:T(8,128)(2,1)S(1)} %shard_map.151), channel_id=1, replica_groups={{0,4,64,68,8,12,72,76,16,20,80,84,24,28,88,92},{1,5,65,69,9,13,73,77,17..., dimensions={0} | all-to-all | bytes 2097152 | tf_op jit(solution)/shard_map/all_to_all | solution.py:54
  128.5 1.4 shard_map.152
  129.9 19.8 %all_to_all.17.own = bf16[16,128,256]{2,1,0:T(8,128)(2,1)S(1)} all-to-all(bf16[16,128,256]{2,1,0:T(8,128)(2,1)S(1)} %get-tuple-element.50), channel_id=1, replica_groups={{0,4,64,68,8,12,72,76,16,20,80,84,24,28,88,92},{1,5,65,69,9,13,73,77,17..., dimensions={0} | all-to-all | bytes 2097152 | tf_op jit(solution)/shard_map/all_to_all | solution.py:54
  149.7 1.5 collective-permute-start.39
  151.1 1.8 collective-permute-start.40
  152.9 1.8 collective-permute-start.41
  157.0 3.3 %collective-permute-start.2 = (f32[8,128]{1,0:T(8,128)S(1)}, f32[8,128]{1,0:T(8,128)S(1)}, u32[]{:S(2)}, u32[]{:S(2)}) collective-permute-start(f32[8,128]{1,0:T(8,128)S(1)} %max.60), channel_id=1, source_target_pairs={{0,68},{1,69},{2,70},{3,71},{8,76},{9,77},{10,78},{11,79},{16,84},... | collective-permute-start | bytes 12296 | tf_op jit(solution)/shard_map/ppermute | solution.py:59
  160.3 1.8 collective-permute-done.3
  162.8 4.2 %collective-permute-done.1 = f32[8,128]{1,0:T(8,128)S(1)} collective-permute-done((f32[8,128]{1,0:T(8,128)S(1)}, f32[8,128]{1,0:T(8,128)S(1)}, u32[]{:S(2)}, u32[]{:S(2)}) %collective-permute-start.1) | collective-permute-done | bytes 4128 | tf_op jit(solution)/shard_map/ppermute | solution.py:59
  167.4 1.9 collective-permute-start.5
  169.3 2.8 %collective-permute-done.6 = f32[8,128]{1,0:T(8,128)S(1)} collective-permute-done((f32[8,128]{1,0:T(8,128)S(1)}, f32[8,128]{1,0:T(8,128)S(1)}, u32[]{:S(2)}, u32[]{:S(2)}) %collective-permute-start.6) | collective-permute-done | bytes 4128 | tf_op jit(solution)/shard_map/ppermute | solution.py:59
  172.2 4.8 %collective-permute-done.4 = f32[8,128]{1,0:T(8,128)S(1)} collective-permute-done((f32[8,128]{1,0:T(8,128)S(1)}, f32[8,128]{1,0:T(8,128)S(1)}, u32[]{:S(2)}, u32[]{:S(2)}) %collective-permute-start.4) | collective-permute-done | bytes 4128 | tf_op jit(solution)/shard_map/ppermute | solution.py:59
  176.9 1.8 collective-permute-start.9
  178.7 1.5 collective-permute-start.8
  182.5 2.7 %collective-permute-start.14 = (bf16[3,3,16,128]{3,2,1,0:T(8,128)(2,1)S(1)}, bf16[3,3,16,128]{3,2,1,0:T(8,128)(2,1)S(1)}, u32[]{:S(2)}, u32[]{:S(2)}) collective-permute-start(bf16[3,3,16,128]{3,2,1,0:T(8,128)(2,1)S(1)} %get-tuple-element.69), channel_id=1, source_target_pairs={{32,0},{64,32},{96,64},{0,96},{33,1},{65,33},{97,65},{1,97},{34,2}... | collective-permute-start | bytes 110600 | tf_op jit(solution)/shard_map/ppermute | solution.py:320
  185.5 6.0 %collective-permute-start.16 = (bf16[3,16,3,128]{3,2,1,0:T(4,128)(2,1)S(1)}, bf16[3,16,3,128]{3,2,1,0:T(4,128)(2,1)S(1)}, u32[]{:S(2)}, u32[]{:S(2)}) collective-permute-start(bf16[3,16,3,128]{3,2,1,0:T(4,128)(2,1)S(1)} %get-tuple-element.67), channel_id=1, source_target_pairs={{1,0},{2,1},{3,2},{4,3},{5,4},{6,5},{7,6},{8,7},{9,8},{10,9},{11,1... | collective-permute-start | bytes 110600 | tf_op jit(solution)/shard_map/ppermute | solution.py:320
  191.5 2.0 collective-permute-done.15
  193.5 8.2 %shard_map.148 = (f32[3,16,16,128]{3,2,1,0:T(8,128)S(1)}, f32[8,128]{1,0:T(8,128)S(1)}) custom-call(f32[8,128]{1,0:T(8,128)S(1)} %maximum_maximum_fusion.3.tops, f32[3,16,16,128]{3,2,1,0:T(8,128)S(1)} %copy-done, f32[3,3,16,128]{3,2,1,0:T(8,128)S(1)} %convert_element_type.31.low_x, f32[3,3,16,128]{3,2,1,0:T(8,128)S(1)} %convert_element_type.32.high_x, ...), custom_call_target="tpu_custom_call" | custom-call | tf_op jit(solution)/shard_map/pallas_call | solution.py:399
  203.6 2.0 collective-permute-start.23
  205.6 2.5 collective-permute-done.25
  208.7 2.1 collective-permute-start.27
  210.8 3.0 %collective-permute-done.28 = f32[8,128]{1,0:T(8,128)S(1)} collective-permute-done((f32[8,128]{1,0:T(8,128)S(1)}, f32[8,128]{1,0:T(8,128)S(1)}, u32[]{:S(2)}, u32[]{:S(2)}) %collective-permute-start.28) | collective-permute-done | bytes 4128 | tf_op jit(solution)/shard_map/ppermute | solution.py:59
  213.8 4.8 %collective-permute-done.26 = f32[8,128]{1,0:T(8,128)S(1)} collective-permute-done((f32[8,128]{1,0:T(8,128)S(1)}, f32[8,128]{1,0:T(8,128)S(1)}, u32[]{:S(2)}, u32[]{:S(2)}) %collective-permute-start.26) | collective-permute-done | bytes 4128 | tf_op jit(solution)/shard_map/ppermute | solution.py:59
  218.6 1.4 collective-permute-start.31
  220.1 4.6 %collective-permute-start.30 = (f32[8,128]{1,0:T(8,128)S(1)}, f32[8,128]{1,0:T(8,128)S(1)}, u32[]{:S(2)}, u32[]{:S(2)}) collective-permute-start(f32[8,128]{1,0:T(8,128)S(1)} %maximum_maximum_fusion.1), channel_id=1, source_target_pairs={{0,3},{1,0},{2,1},{3,2},{8,11},{9,8},{10,9},{11,10},{16,19},{17,16... | collective-permute-start | bytes 12296 | tf_op jit(solution)/shard_map/ppermute | solution.py:59
  224.6 2.3 collective-permute-start.29
  227.1 4.1 %collective-permute-done.29 = f32[8,128]{1,0:T(8,128)S(1)} collective-permute-done((f32[8,128]{1,0:T(8,128)S(1)}, f32[8,128]{1,0:T(8,128)S(1)}, u32[]{:S(2)}, u32[]{:S(2)}) %collective-permute-start.29) | collective-permute-done | bytes 4128 | tf_op jit(solution)/shard_map/ppermute | solution.py:59
  232.3 1.7 collective-permute-start.37
  234.0 4.6 %collective-permute-start.38 = (bf16[3,16,3,128]{3,2,1,0:T(4,128)(2,1)S(1)}, bf16[3,16,3,128]{3,2,1,0:T(4,128)(2,1)S(1)}, u32[]{:S(2)}, u32[]{:S(2)}) collective-permute-start(bf16[3,16,3,128]{3,2,1,0:T(4,128)(2,1)S(1)} %get-tuple-element.63), channel_id=1, source_target_pairs={{1,0},{2,1},{3,2},{4,3},{5,4},{6,5},{7,6},{8,7},{9,8},{10,9},{11,1... | collective-permute-start | bytes 110600 | tf_op jit(solution)/shard_map/ppermute | solution.py:320
  238.6 2.0 collective-permute-done.37
  240.7 8.8 %shard_map.153 = (f32[3,16,16,128]{3,2,1,0:T(8,128)S(1)}, f32[8,128]{1,0:T(8,128)}) custom-call(f32[8,128]{1,0:T(8,128)S(1)} %maximum_maximum_fusion.tops, f32[3,16,16,128]{3,2,1,0:T(8,128)S(1)} %get-tuple-element.52.field, f32[3,3,16,128]{3,2,1,0:T(8,128)S(1)} %convert_element_type.36.low_x, f32[3,3,16,128]{3,2,1,0:T(8,128)S(1)} %convert_element_type.37.high_x, ...), custom_call_target="tpu_custom_call" | custom-call | tf_op jit(solution)/shard_map/pallas_call | solution.py:399
  249.5 4.1 %shard_map.155 = f32[3,16,16,128]{3,2,1,0:T(8,128)} custom-call(s32[5]{0:T(128)S(1)} %stack.23.place, bf16[64,1536]{1,0:T(8,128)(2,1)S(1)} %get-tuple-element.35.patches, f32[3,16,16,128]{3,2,1,0:T(8,128)S(1)} %get-tuple-element.53.field, bf16[2,1536,256]{2,1,0:T(8,128)(2,1)S(1)} %get-tuple-element.54.m1, bf16[2,1024,256]{2,1,0:T(8,128)(2,1)S(1)} %get-tuple-element.55.m2, ...), custom_call_target="tpu_custom_call" | custom-call | tf_op jit(solution)/shard_map/pallas_call | solution.py:88
  (107 shorter events, 20.9 us)
Async XLA Ops:
  29.4 30.6 %copy-start.12 = (s32[128]{0:T(128)S(1)}, s32[128]{0:T(128)}, u32[]{:S(2)}) copy-start(s32[128]{0:T(128)} %param.16) | copy-start | bytes 1540
  29.4 31.4 %copy-start = (f32[3,16,16,128]{3,2,1,0:T(8,128)S(1)}, f32[3,16,16,128]{3,2,1,0:T(8,128)}, u32[]{:S(2)}) copy-start(f32[3,16,16,128]{3,2,1,0:T(8,128)} %field.5) | copy-start | bytes 1179652
  29.4 16.0 %collective-permute-start.10 = (bf16[16,128,256]{2,1,0:T(8,128)(2,1)S(1)}, bf16[16,128,256]{2,1,0:T(8,128)(2,1)S(1)}, u32[]{:S(2)}, u32[]{:S(2)}) collective-permute-start(bf16[16,128,256]{2,1,0:T(8,128)(2,1)S(1)} %all_to_all.15.own), channel_id=1, source_target_pairs={{0,1},{1,2},{2,3},{3,0},{8,9},{9,10},{10,11},{11,8},{16,17},{17,18... | collective-permute-start | bytes 3145736 | tf_op jit(solution)/shard_map/ppermute | solution.py:59
  30.9 25.4 %collective-permute-start.11 = (bf16[16,128,256]{2,1,0:T(8,128)(2,1)S(1)}, bf16[16,128,256]{2,1,0:T(8,128)(2,1)S(1)}, u32[]{:S(2)}, u32[]{:S(2)}) collective-permute-start(bf16[16,128,256]{2,1,0:T(8,128)(2,1)S(1)} %all_to_all.15.own), channel_id=1, source_target_pairs={{0,3},{1,0},{2,1},{3,2},{8,11},{9,8},{10,9},{11,10},{16,19},{17,16... | collective-permute-start | bytes 3145736 | tf_op jit(solution)/shard_map/ppermute | solution.py:59
  32.7 24.9 %collective-permute-start.12 = (bf16[16,128,256]{2,1,0:T(8,128)(2,1)S(1)}, bf16[16,128,256]{2,1,0:T(8,128)(2,1)S(1)}, u32[]{:S(2)}, u32[]{:S(2)}) collective-permute-start(bf16[16,128,256]{2,1,0:T(8,128)(2,1)S(1)} %all_to_all.15.own), channel_id=1, source_target_pairs={{0,2},{1,3},{2,0},{3,1},{8,10},{9,11},{10,8},{11,9},{16,18},{17,19... | collective-permute-start | bytes 3145736 | tf_op jit(solution)/shard_map/ppermute | solution.py:59
  59.5 7.3 %collective-permute-start.17 = (bf16[2,1536,256]{2,1,0:T(8,128)(2,1)S(1)}, bf16[2,1536,256]{2,1,0:T(8,128)(2,1)}, u32[]{:S(2)}, u32[]{:S(2)}) collective-permute-start(bf16[2,1536,256]{2,1,0:T(8,128)(2,1)S(1)} %get-tuple-element.36.m1), channel_id=1, source_target_pairs={{0,32},{32,0},{1,33},{33,1},{2,34},{34,2},{3,35},{35,3},{4,36},{36... | collective-permute-start | bytes 4718600 | tf_op jit(solution)/shard_map/ppermute | solution.py:63
  59.6 7.3 %collective-permute-start.19 = (bf16[2,1536,256]{2,1,0:T(8,128)(2,1)S(1)}, bf16[2,1536,256]{2,1,0:T(8,128)(2,1)}, u32[]{:S(2)}, u32[]{:S(2)}) collective-permute-start(bf16[2,1536,256]{2,1,0:T(8,128)(2,1)S(1)} %get-tuple-element.42.m3), channel_id=1, source_target_pairs={{0,32},{32,0},{1,33},{33,1},{2,34},{34,2},{3,35},{35,3},{4,36},{36... | collective-permute-start | bytes 4718600 | tf_op jit(solution)/shard_map/ppermute | solution.py:63
  60.1 6.8 %collective-permute-start.18 = (bf16[2,1024,256]{2,1,0:T(8,128)(2,1)}, bf16[2,1024,256]{2,1,0:T(8,128)(2,1)}, u32[]{:S(2)}, u32[]{:S(2)}) collective-permute-start(bf16[2,1024,256]{2,1,0:T(8,128)(2,1)} %get-tuple-element.41.m2), channel_id=1, source_target_pairs={{0,32},{32,0},{1,33},{33,1},{2,34},{34,2},{3,35},{35,3},{4,36},{36... | collective-permute-start | bytes 3145736 | tf_op jit(solution)/shard_map/ppermute | solution.py:63
  74.3 3.3 %collective-permute-start.20 = (bf16[128,4096]{1,0:T(8,128)(2,1)S(1)}, bf16[128,4096]{1,0:T(8,128)(2,1)S(1)}, u32[]{:S(2)}, u32[]{:S(2)}) collective-permute-start(bf16[128,4096]{1,0:T(8,128)(2,1)S(1)} %get-tuple-element.44), channel_id=1, source_target_pairs={{0,32},{32,0},{1,33},{33,1},{2,34},{34,2},{3,35},{35,3},{4,36},{36... | collective-permute-start | bytes 3145736 | tf_op jit(solution)/shard_map/ppermute | solution.py:63
  74.6 3.1 %collective-permute-start.21 = (bf16[128,1536]{1,0:T(8,128)(2,1)S(1)}, bf16[128,1536]{1,0:T(8,128)(2,1)S(1)}, u32[]{:S(2)}, u32[]{:S(2)}) collective-permute-start(bf16[128,1536]{1,0:T(8,128)(2,1)S(1)} %get-tuple-element.40.picked), channel_id=1, source_target_pairs={{0,32},{32,0},{1,33},{33,1},{2,34},{34,2},{3,35},{35,3},{4,36},{36... | collective-permute-start | bytes 1179656 | tf_op jit(solution)/shard_map/ppermute | solution.py:63
  79.7 16.1 %collective-permute-start.32 = (bf16[16,128,256]{2,1,0:T(8,128)(2,1)S(1)}, bf16[16,128,256]{2,1,0:T(8,128)(2,1)S(1)}, u32[]{:S(2)}, u32[]{:S(2)}) collective-permute-start(bf16[16,128,256]{2,1,0:T(8,128)(2,1)S(1)} %get-tuple-element.48), channel_id=1, source_target_pairs={{0,1},{1,2},{2,3},{3,0},{8,9},{9,10},{10,11},{11,8},{16,17},{17,18... | collective-permute-start | bytes 3145736 | tf_op jit(solution)/shard_map/ppermute | solution.py:59
  81.2 25.4 %collective-permute-start.33 = (bf16[16,128,256]{2,1,0:T(8,128)(2,1)S(1)}, bf16[16,128,256]{2,1,0:T(8,128)(2,1)S(1)}, u32[]{:S(2)}, u32[]{:S(2)}) collective-permute-start(bf16[16,128,256]{2,1,0:T(8,128)(2,1)S(1)} %get-tuple-element.45), channel_id=1, source_target_pairs={{0,3},{1,0},{2,1},{3,2},{8,11},{9,8},{10,9},{11,10},{16,19},{17,16... | collective-permute-start | bytes 3145736 | tf_op jit(solution)/shard_map/ppermute | solution.py:59
  83.0 24.6 %collective-permute-start.34 = (bf16[16,128,256]{2,1,0:T(8,128)(2,1)S(1)}, bf16[16,128,256]{2,1,0:T(8,128)(2,1)S(1)}, u32[]{:S(2)}, u32[]{:S(2)}) collective-permute-start(bf16[16,128,256]{2,1,0:T(8,128)(2,1)S(1)} %get-tuple-element.49), channel_id=1, source_target_pairs={{0,2},{1,3},{2,0},{3,1},{8,10},{9,11},{10,8},{11,9},{16,18},{17,19... | collective-permute-start | bytes 3145736 | tf_op jit(solution)/shard_map/ppermute | solution.py:59
  108.7 19.7 %copy-start.2 = (f32[48,1024]{1,0:T(8,128)S(1)}, f32[48,1024]{1,0:T(8,128)}, u32[]{:S(2)}) copy-start(f32[48,1024]{1,0:T(8,128)} %refs_0_.1) | copy-start | bytes 589828
  149.7 29.1 %collective-permute-start.39 = (bf16[16,128,256]{2,1,0:T(8,128)(2,1)S(1)}, bf16[16,128,256]{2,1,0:T(8,128)(2,1)S(1)}, u32[]{:S(2)}, u32[]{:S(2)}) collective-permute-start(bf16[16,128,256]{2,1,0:T(8,128)(2,1)S(1)} %all_to_all.17.own), channel_id=1, source_target_pairs={{0,1},{1,2},{2,3},{3,0},{8,9},{9,10},{10,11},{11,8},{16,17},{17,18... | collective-permute-start | bytes 3145736 | tf_op jit(solution)/shard_map/ppermute | solution.py:59
  151.1 29.1 %collective-permute-start.40 = (bf16[16,128,256]{2,1,0:T(8,128)(2,1)S(1)}, bf16[16,128,256]{2,1,0:T(8,128)(2,1)S(1)}, u32[]{:S(2)}, u32[]{:S(2)}) collective-permute-start(bf16[16,128,256]{2,1,0:T(8,128)(2,1)S(1)} %all_to_all.17.own), channel_id=1, source_target_pairs={{0,3},{1,0},{2,1},{3,2},{8,11},{9,8},{10,9},{11,10},{16,19},{17,16... | collective-permute-start | bytes 3145736 | tf_op jit(solution)/shard_map/ppermute | solution.py:59
  152.9 27.9 %collective-permute-start.41 = (bf16[16,128,256]{2,1,0:T(8,128)(2,1)S(1)}, bf16[16,128,256]{2,1,0:T(8,128)(2,1)S(1)}, u32[]{:S(2)}, u32[]{:S(2)}) collective-permute-start(bf16[16,128,256]{2,1,0:T(8,128)(2,1)S(1)} %all_to_all.17.own), channel_id=1, source_target_pairs={{0,2},{1,3},{2,0},{3,1},{8,10},{9,11},{10,8},{11,9},{16,18},{17,19... | collective-permute-start | bytes 3145736 | tf_op jit(solution)/shard_map/ppermute | solution.py:59
  155.8 1.2 collective-permute-start
  157.0 5.1 %collective-permute-start.3 = (f32[8,128]{1,0:T(8,128)S(1)}, f32[8,128]{1,0:T(8,128)S(1)}, u32[]{:S(2)}, u32[]{:S(2)}) collective-permute-start(f32[8,128]{1,0:T(8,128)S(1)} %max.60), channel_id=1, source_target_pairs={{0,64},{1,65},{2,66},{3,67},{8,72},{9,73},{10,74},{11,75},{16,80},... | collective-permute-start | bytes 12296 | tf_op jit(solution)/shard_map/ppermute | solution.py:59
  157.0 5.7 %collective-permute-start.2 = (f32[8,128]{1,0:T(8,128)S(1)}, f32[8,128]{1,0:T(8,128)S(1)}, u32[]{:S(2)}, u32[]{:S(2)}) collective-permute-start(f32[8,128]{1,0:T(8,128)S(1)} %max.60), channel_id=1, source_target_pairs={{0,68},{1,69},{2,70},{3,71},{8,76},{9,77},{10,78},{11,79},{16,84},... | collective-permute-start | bytes 12296 | tf_op jit(solution)/shard_map/ppermute | solution.py:59
  162.1 4.8 %collective-permute-start.1 = (f32[8,128]{1,0:T(8,128)S(1)}, f32[8,128]{1,0:T(8,128)S(1)}, u32[]{:S(2)}, u32[]{:S(2)}) collective-permute-start(f32[8,128]{1,0:T(8,128)S(1)} %max.60), channel_id=1, source_target_pairs={{0,4},{1,5},{2,6},{3,7},{8,12},{9,13},{10,14},{11,15},{16,20},{17,... | collective-permute-start | bytes 12296 | tf_op jit(solution)/shard_map/ppermute | solution.py:59
  167.0 5.2 %collective-permute-start.6 = (f32[8,128]{1,0:T(8,128)S(1)}, f32[8,128]{1,0:T(8,128)S(1)}, u32[]{:S(2)}, u32[]{:S(2)}) collective-permute-start(f32[8,128]{1,0:T(8,128)S(1)} %maximum_maximum_fusion.5), channel_id=1, source_target_pairs={{0,16},{1,17},{2,18},{3,19},{8,24},{9,25},{10,26},{11,27},{16,0},{... | collective-permute-start | bytes 12296 | tf_op jit(solution)/shard_map/ppermute | solution.py:59
  167.4 4.8 %collective-permute-start.5 = (f32[8,128]{1,0:T(8,128)S(1)}, f32[8,128]{1,0:T(8,128)S(1)}, u32[]{:S(2)}, u32[]{:S(2)}) collective-permute-start(f32[8,128]{1,0:T(8,128)S(1)} %maximum_maximum_fusion.5), channel_id=1, source_target_pairs={{0,24},{1,25},{2,26},{3,27},{8,0},{9,1},{10,2},{11,3},{16,8},{17,9... | collective-permute-start | bytes 12296 | tf_op jit(solution)/shard_map/ppermute | solution.py:59
  172.1 4.8 %collective-permute-start.4 = (f32[8,128]{1,0:T(8,128)S(1)}, f32[8,128]{1,0:T(8,128)S(1)}, u32[]{:S(2)}, u32[]{:S(2)}) collective-permute-start(f32[8,128]{1,0:T(8,128)S(1)} %maximum_maximum_fusion.5), channel_id=1, source_target_pairs={{0,8},{1,9},{2,10},{3,11},{8,16},{9,17},{10,18},{11,19},{16,24},{1... | collective-permute-start | bytes 12296 | tf_op jit(solution)/shard_map/ppermute | solution.py:59
  176.9 5.1 %collective-permute-start.9 = (f32[8,128]{1,0:T(8,128)S(1)}, f32[8,128]{1,0:T(8,128)S(1)}, u32[]{:S(2)}, u32[]{:S(2)}) collective-permute-start(f32[8,128]{1,0:T(8,128)S(1)} %maximum_maximum_fusion.4), channel_id=1, source_target_pairs={{0,2},{1,3},{2,0},{3,1},{8,10},{9,11},{10,8},{11,9},{16,18},{17,19... | collective-permute-start | bytes 12296 | tf_op jit(solution)/shard_map/ppermute | solution.py:59
  178.7 6.7 %collective-permute-start.13 = (bf16[3,3,16,128]{3,2,1,0:T(8,128)(2,1)S(1)}, bf16[3,3,16,128]{3,2,1,0:T(8,128)(2,1)S(1)}, u32[]{:S(2)}, u32[]{:S(2)}) collective-permute-start(bf16[3,3,16,128]{3,2,1,0:T(8,128)(2,1)S(1)} %get-tuple-element.70), channel_id=1, source_target_pairs={{0,32},{32,64},{64,96},{96,0},{1,33},{33,65},{65,97},{97,1},{2,34}... | collective-permute-start | bytes 110600 | tf_op jit(solution)/shard_map/ppermute | solution.py:319
  178.7 3.8 %collective-permute-start.8 = (f32[8,128]{1,0:T(8,128)S(1)}, f32[8,128]{1,0:T(8,128)S(1)}, u32[]{:S(2)}, u32[]{:S(2)}) collective-permute-start(f32[8,128]{1,0:T(8,128)S(1)} %maximum_maximum_fusion.4), channel_id=1, source_target_pairs={{0,3},{1,0},{2,1},{3,2},{8,11},{9,8},{10,9},{11,10},{16,19},{17,16... | collective-permute-start | bytes 12296 | tf_op jit(solution)/shard_map/ppermute | solution.py:59
  180.2 5.0 %collective-permute-start.7 = (f32[8,128]{1,0:T(8,128)S(1)}, f32[8,128]{1,0:T(8,128)S(1)}, u32[]{:S(2)}, u32[]{:S(2)}) collective-permute-start(f32[8,128]{1,0:T(8,128)S(1)} %maximum_maximum_fusion.4), channel_id=1, source_target_pairs={{0,1},{1,2},{2,3},{3,0},{8,9},{9,10},{10,11},{11,8},{16,17},{17,18... | collective-permute-start | bytes 12296 | tf_op jit(solution)/shard_map/ppermute | solution.py:59
  181.9 67.6 %collective-permute-start.42 = (bf16[2,1536,256]{2,1,0:T(8,128)(2,1)S(1)}, bf16[2,1536,256]{2,1,0:T(8,128)(2,1)S(1)}, u32[]{:S(2)}, u32[]{:S(2)}) collective-permute-start(bf16[2,1536,256]{2,1,0:T(8,128)(2,1)S(1)} %get-tuple-element.54.m1), channel_id=1, source_target_pairs={{0,32},{32,0},{1,33},{33,1},{2,34},{34,2},{3,35},{35,3},{4,36},{36... | collective-permute-start | bytes 4718600 | tf_op jit(solution)/shard_map/ppermute | solution.py:63
  182.1 67.4 %collective-permute-start.44 = (bf16[2,1536,256]{2,1,0:T(8,128)(2,1)S(1)}, bf16[2,1536,256]{2,1,0:T(8,128)(2,1)S(1)}, u32[]{:S(2)}, u32[]{:S(2)}) collective-permute-start(bf16[2,1536,256]{2,1,0:T(8,128)(2,1)S(1)} %get-tuple-element.56.m3), channel_id=1, source_target_pairs={{0,32},{32,0},{1,33},{33,1},{2,34},{34,2},{3,35},{35,3},{4,36},{36... | collective-permute-start | bytes 4718600 | tf_op jit(solution)/shard_map/ppermute | solution.py:63
  182.5 8.9 %collective-permute-start.14 = (bf16[3,3,16,128]{3,2,1,0:T(8,128)(2,1)S(1)}, bf16[3,3,16,128]{3,2,1,0:T(8,128)(2,1)S(1)}, u32[]{:S(2)}, u32[]{:S(2)}) collective-permute-start(bf16[3,3,16,128]{3,2,1,0:T(8,128)(2,1)S(1)} %get-tuple-element.69), channel_id=1, source_target_pairs={{32,0},{64,32},{96,64},{0,96},{33,1},{65,33},{97,65},{1,97},{34,2}... | collective-permute-start | bytes 110600 | tf_op jit(solution)/shard_map/ppermute | solution.py:320
  185.2 8.3 %collective-permute-start.15 = (bf16[3,16,3,128]{3,2,1,0:T(4,128)(2,1)S(1)}, bf16[3,16,3,128]{3,2,1,0:T(4,128)(2,1)S(1)}, u32[]{:S(2)}, u32[]{:S(2)}) collective-permute-start(bf16[3,16,3,128]{3,2,1,0:T(4,128)(2,1)S(1)} %get-tuple-element.68), channel_id=1, source_target_pairs={{0,1},{1,2},{2,3},{3,4},{4,5},{5,6},{6,7},{7,8},{8,9},{9,10},{10,1... | collective-permute-start | bytes 110600 | tf_op jit(solution)/shard_map/ppermute | solution.py:319
  185.5 8.1 %collective-permute-start.16 = (bf16[3,16,3,128]{3,2,1,0:T(4,128)(2,1)S(1)}, bf16[3,16,3,128]{3,2,1,0:T(4,128)(2,1)S(1)}, u32[]{:S(2)}, u32[]{:S(2)}) collective-permute-start(bf16[3,16,3,128]{3,2,1,0:T(4,128)(2,1)S(1)} %get-tuple-element.67), channel_id=1, source_target_pairs={{1,0},{2,1},{3,2},{4,3},{5,4},{6,5},{7,6},{8,7},{9,8},{10,9},{11,1... | collective-permute-start | bytes 110600 | tf_op jit(solution)/shard_map/ppermute | solution.py:320
  201.7 1.2 collective-permute-start.22
  203.0 5.1 %collective-permute-start.25 = (f32[8,128]{1,0:T(8,128)S(1)}, f32[8,128]{1,0:T(8,128)S(1)}, u32[]{:S(2)}, u32[]{:S(2)}) collective-permute-start(f32[8,128]{1,0:T(8,128)S(1)} %max.70), channel_id=1, source_target_pairs={{0,64},{1,65},{2,66},{3,67},{8,72},{9,73},{10,74},{11,75},{16,80},... | collective-permute-start | bytes 12296 | tf_op jit(solution)/shard_map/ppermute | solution.py:59
  203.6 4.5 %collective-permute-start.24 = (f32[8,128]{1,0:T(8,128)S(1)}, f32[8,128]{1,0:T(8,128)S(1)}, u32[]{:S(2)}, u32[]{:S(2)}) collective-permute-start(f32[8,128]{1,0:T(8,128)S(1)} %max.70), channel_id=1, source_target_pairs={{0,68},{1,69},{2,70},{3,71},{8,76},{9,77},{10,78},{11,79},{16,84},... | collective-permute-start | bytes 12296 | tf_op jit(solution)/shard_map/ppermute | solution.py:59
  203.6 5.0 %collective-permute-start.23 = (f32[8,128]{1,0:T(8,128)S(1)}, f32[8,128]{1,0:T(8,128)S(1)}, u32[]{:S(2)}, u32[]{:S(2)}) collective-permute-start(f32[8,128]{1,0:T(8,128)S(1)} %max.70), channel_id=1, source_target_pairs={{0,4},{1,5},{2,6},{3,7},{8,12},{9,13},{10,14},{11,15},{16,20},{17,... | collective-permute-start | bytes 12296 | tf_op jit(solution)/shard_map/ppermute | solution.py:59
  208.1 41.4 %collective-permute-start.43 = (bf16[2,1024,256]{2,1,0:T(8,128)(2,1)S(1)}, bf16[2,1024,256]{2,1,0:T(8,128)(2,1)S(1)}, u32[]{:S(2)}, u32[]{:S(2)}) collective-permute-start(bf16[2,1024,256]{2,1,0:T(8,128)(2,1)S(1)} %get-tuple-element.55.m2), channel_id=1, source_target_pairs={{0,32},{32,0},{1,33},{33,1},{2,34},{34,2},{3,35},{35,3},{4,36},{36... | collective-permute-start | bytes 3145736 | tf_op jit(solution)/shard_map/ppermute | solution.py:63
  208.7 5.1 %collective-permute-start.28 = (f32[8,128]{1,0:T(8,128)S(1)}, f32[8,128]{1,0:T(8,128)S(1)}, u32[]{:S(2)}, u32[]{:S(2)}) collective-permute-start(f32[8,128]{1,0:T(8,128)S(1)} %maximum_maximum_fusion.2), channel_id=1, source_target_pairs={{0,16},{1,17},{2,18},{3,19},{8,24},{9,25},{10,26},{11,27},{16,0},{... | collective-permute-start | bytes 12296 | tf_op jit(solution)/shard_map/ppermute | solution.py:59
  208.7 5.1 %collective-permute-start.27 = (f32[8,128]{1,0:T(8,128)S(1)}, f32[8,128]{1,0:T(8,128)S(1)}, u32[]{:S(2)}, u32[]{:S(2)}) collective-permute-start(f32[8,128]{1,0:T(8,128)S(1)} %maximum_maximum_fusion.2), channel_id=1, source_target_pairs={{0,24},{1,25},{2,26},{3,27},{8,0},{9,1},{10,2},{11,3},{16,8},{17,9... | collective-permute-start | bytes 12296 | tf_op jit(solution)/shard_map/ppermute | solution.py:59
  213.8 4.8 %collective-permute-start.26 = (f32[8,128]{1,0:T(8,128)S(1)}, f32[8,128]{1,0:T(8,128)S(1)}, u32[]{:S(2)}, u32[]{:S(2)}) collective-permute-start(f32[8,128]{1,0:T(8,128)S(1)} %maximum_maximum_fusion.2), channel_id=1, source_target_pairs={{0,8},{1,9},{2,10},{3,11},{8,16},{9,17},{10,18},{11,19},{16,24},{1... | collective-permute-start | bytes 12296 | tf_op jit(solution)/shard_map/ppermute | solution.py:59
  218.6 6.0 %collective-permute-start.31 = (f32[8,128]{1,0:T(8,128)S(1)}, f32[8,128]{1,0:T(8,128)S(1)}, u32[]{:S(2)}, u32[]{:S(2)}) collective-permute-start(f32[8,128]{1,0:T(8,128)S(1)} %maximum_maximum_fusion.1), channel_id=1, source_target_pairs={{0,2},{1,3},{2,0},{3,1},{8,10},{9,11},{10,8},{11,9},{16,18},{17,19... | collective-permute-start | bytes 12296 | tf_op jit(solution)/shard_map/ppermute | solution.py:59
  220.1 7.0 %collective-permute-start.30 = (f32[8,128]{1,0:T(8,128)S(1)}, f32[8,128]{1,0:T(8,128)S(1)}, u32[]{:S(2)}, u32[]{:S(2)}) collective-permute-start(f32[8,128]{1,0:T(8,128)S(1)} %maximum_maximum_fusion.1), channel_id=1, source_target_pairs={{0,3},{1,0},{2,1},{3,2},{8,11},{9,8},{10,9},{11,10},{16,19},{17,16... | collective-permute-start | bytes 12296 | tf_op jit(solution)/shard_map/ppermute | solution.py:59
  224.6 6.6 %collective-permute-start.29 = (f32[8,128]{1,0:T(8,128)S(1)}, f32[8,128]{1,0:T(8,128)S(1)}, u32[]{:S(2)}, u32[]{:S(2)}) collective-permute-start(f32[8,128]{1,0:T(8,128)S(1)} %maximum_maximum_fusion.1), channel_id=1, source_target_pairs={{0,1},{1,2},{2,3},{3,0},{8,9},{9,10},{10,11},{11,8},{16,17},{17,18... | collective-permute-start | bytes 12296 | tf_op jit(solution)/shard_map/ppermute | solution.py:59
  227.1 5.2 %collective-permute-start.35 = (bf16[3,3,16,128]{3,2,1,0:T(8,128)(2,1)S(1)}, bf16[3,3,16,128]{3,2,1,0:T(8,128)(2,1)S(1)}, u32[]{:S(2)}, u32[]{:S(2)}) collective-permute-start(bf16[3,3,16,128]{3,2,1,0:T(8,128)(2,1)S(1)} %get-tuple-element.66), channel_id=1, source_target_pairs={{0,32},{32,64},{64,96},{96,0},{1,33},{33,65},{65,97},{97,1},{2,34}... | collective-permute-start | bytes 110600 | tf_op jit(solution)/shard_map/ppermute | solution.py:319
  231.2 2.8 %collective-permute-start.36 = (bf16[3,3,16,128]{3,2,1,0:T(8,128)(2,1)S(1)}, bf16[3,3,16,128]{3,2,1,0:T(8,128)(2,1)S(1)}, u32[]{:S(2)}, u32[]{:S(2)}) collective-permute-start(bf16[3,3,16,128]{3,2,1,0:T(8,128)(2,1)S(1)} %get-tuple-element.65), channel_id=1, source_target_pairs={{32,0},{64,32},{96,64},{0,96},{33,1},{65,33},{97,65},{1,97},{34,2}... | collective-permute-start | bytes 110600 | tf_op jit(solution)/shard_map/ppermute | solution.py:320
  232.3 8.3 %collective-permute-start.37 = (bf16[3,16,3,128]{3,2,1,0:T(4,128)(2,1)S(1)}, bf16[3,16,3,128]{3,2,1,0:T(4,128)(2,1)S(1)}, u32[]{:S(2)}, u32[]{:S(2)}) collective-permute-start(bf16[3,16,3,128]{3,2,1,0:T(4,128)(2,1)S(1)} %get-tuple-element.64), channel_id=1, source_target_pairs={{0,1},{1,2},{2,3},{3,4},{4,5},{5,6},{6,7},{7,8},{8,9},{9,10},{10,1... | collective-permute-start | bytes 110600 | tf_op jit(solution)/shard_map/ppermute | solution.py:319
  234.0 6.6 %collective-permute-start.38 = (bf16[3,16,3,128]{3,2,1,0:T(4,128)(2,1)S(1)}, bf16[3,16,3,128]{3,2,1,0:T(4,128)(2,1)S(1)}, u32[]{:S(2)}, u32[]{:S(2)}) collective-permute-start(bf16[3,16,3,128]{3,2,1,0:T(4,128)(2,1)S(1)} %get-tuple-element.63), channel_id=1, source_target_pairs={{1,0},{2,1},{3,2},{4,3},{5,4},{6,5},{7,6},{8,7},{9,8},{10,9},{11,1... | collective-permute-start | bytes 110600 | tf_op jit(solution)/shard_map/ppermute | solution.py:320
  (10 other events, 103.2 us)
where the time goes:
time: 254 us
  waiting for transfers between devices  89.1 us (35%)
  blocking collectives  64.7 us (25%)
  starting transfers between devices  54 us (21%)
  Pallas kernels  39 us (15%)
  local copies, waits for them, and re-layouts  5.56 us (2%)
    ppermute x27, waiting for transfers between devices, spread(): lax.ppermute(take(s), AXES, phase_pairs(phase, s))  76 us
    all_to_all x3, blocking collectives, exchange_planes(): lax.all_to_all(blocks, AXES, 0, 0, tiled=True, axis_index_groups=planes())  64.7 us
    ppermute x27, starting transfers between devices, spread(): lax.ppermute(take(s), AXES, phase_pairs(phase, s))  37.1 us
    pallas_call x10, Pallas kernels, call(): pl.pallas_call(kernel, out_shape=outs, in_specs=[SMEM] + [VMEM] * len(arr...  22 us
    pallas_call x2, Pallas kernels, advect(): pl.pallas_call(advect_kernel, out_shape=(like(field.shape, f32), like((8,...  17 us
    ppermute x4, starting transfers between devices, edges_of(): lax.ppermute(leading, axis, [(b, a) for a, b in up]).astype(f32)  13.2 us
    ppermute x10, waiting for transfers between devices, swap_cores(): return lax.ppermute(array, 'role_1', [(0, 1), (1, 0)])  8.07 us
    ppermute x4, waiting for transfers between devices, edges_of(): found.append(lax.ppermute(last, axis, up).astype(f32))  5.08 us
  transfers between devices with their start and end apart: 45, of which 24 were waited for; matrix products, arithmetic and copies ran while one was open for 0% of the time, Pallas kernels for 8%

commit v1 on v0

--- a/solution.py
+++ b/solution.py
@@ -72,7 +72,8 @@
     second = jnp.where(core == 0, y, x)
     third = jnp.where(core == 0, z, y)
     role = lax.axis_index(ROLE)
-    return jnp.stack([core, first, second, third, role]).astype(jnp.int32)
+    beside = jnp.where(core == 0, y, z)
+    return jnp.stack([core, first, second, third, role, beside]).astype(jnp.int32)
 
 
 VMEM = pl.BlockSpec(memory_space=pltpu.VMEM)
@@ -100,33 +101,69 @@
 
 
 def own_block_kernel(place, first, middle, last, out):
-    cols = pl.ds(pl.multiple_of(place[4] * LANES, LANES), LANES)
     for ref, start, rows in zip((first, middle, last), STARTS, ROWS):
-        part = ref[:, cols].astype(bf16)
+        part = ref[...].astype(bf16)
         for copy in range(16):
             out[copy, start : start + rows, :] = part
 
 
-def finish_kernel(place, own, one, three, two, first, middle, last):
-    core, mine = place[0], place[3]
-    for s, ref in ((0, own), (1, one), (3, three), (2, two)):
-        at3 = lax.rem(mine + 4 - s, 4)
-        for at2 in range(4):
-            for at1 in range(4):
-                x = jnp.where(core == 0, at1, at2)
-                y = jnp.where(core == 0, at2, at3)
-                z = jnp.where(core == 0, at3, at1)
-                high = x // 2
-                brick = y * 8 + (x - high * 2) * 4 + z
-                for out, start, rows in zip((first, middle, last), STARTS, ROWS):
-                    to = pl.ds(pl.multiple_of(brick * rows, 16), rows)
-                    out[high, to, :] = ref[at2 * 4 + at1, start : start + rows, :]
+def own_block(place, layers):
+    grid = pltpu.PrefetchScalarGridSpec(
+        num_scalar_prefetch=1,
+        grid=(1,),
+        in_specs=[pl.BlockSpec((rows, LANES), lambda i, place: (0, place[4])) for rows in ROWS],
+        out_specs=pl.BlockSpec((16, BLOCK, LANES), lambda i, place: (0, 0, 0)),
+    )
+    return pl.pallas_call(
+        own_block_kernel,
+        out_shape=like((16, BLOCK, LANES), bf16),
+        grid_spec=grid,
+        compiler_params=pltpu.CompilerParams(vmem_limit_bytes=8 << 20),
+        name="own_block",
+    )(place, *layers)
+
+
+def finish_kernel(of_other):
+    def kernel(place, own, one, three, low, high_part, first, middle, last):
+        core = 1 - place[0] if of_other else place[0]
+        mine = place[5] if of_other else place[3]
+        for s, ref in ((0, own), (1, one), (3, three), (2, None)):
+            at3 = lax.rem(mine + 4 - s, 4)
+            for at2 in range(4):
+                for at1 in range(4):
+                    n = at2 * 4 + at1
+                    source, at = (ref, n) if ref is not None else ((low, n) if n < 8 else (high_part, n - 8))
+                    x = jnp.where(core == 0, at1, at2)
+                    y = jnp.where(core == 0, at2, at3)
+                    z = jnp.where(core == 0, at3, at1)
+                    high = x // 2
+                    brick = y * 8 + (x - high * 2) * 4 + z
+                    for out, start, rows in zip((first, middle, last), STARTS, ROWS):
+                        to = pl.ds(pl.multiple_of(brick * rows, 16), rows)
+                        out[high, to, :] = source[at, start : start + rows, :]
+
+    return kernel
 
 
 def gather_matrices(square, place):
-    got = spread(square, 2)
-    mine = call(finish_kernel, tuple(like((2, 32 * rows, LANES), bf16) for rows in ROWS), place, square, *got)
-    return mine, tuple(swap_cores(m) for m in mine)
+    def shifted(array, shift):
+        return lax.ppermute(array, AXES, phase_pairs(2, shift))
+
+    def finish(pieces, of_other):
+        return call(
+            finish_kernel(of_other),
+            tuple(like((2, 32 * rows, LANES), bf16) for rows in ROWS),
+            place,
+            *pieces,
+        )
+
+    one, three = shifted(square, 1), shifted(square, 3)
+    given = [swap_cores(square)]
+    low, high = shifted(one[:8], 1), shifted(three[8:], 3)
+    given += [swap_cores(one), swap_cores(three)]
+    given += [swap_cores(low), swap_cores(high)]
+    mine = finish((square, one, three, low, high), False)
+    return mine, finish(given, True)
 
 
 def swap_blocks(tile):
@@ -429,12 +466,16 @@
 def whole(velocity, first, middle, last, first_moment, middle_moment, last_moment, patch_pick, targets):
     place = places()
     layers, moments = (first, middle, last), (first_moment, middle_moment, last_moment)
-    copies = call(own_block_kernel, like((16, BLOCK, LANES), bf16), place, *layers)
+    copies = own_block(place, layers)
     square = exchange_planes(copies)
     mine, other = gather_matrices(square, place)
     top = call(top_kernel, like((8, 128), f32), place, velocity)
     patches, chosen = call(
-        cut_kernel, (like((64, 1536), bf16), like((BLOCK, 1536), bf16)), place, velocity, patch_pick.reshape(BLOCK, 1)
+        cut_kernel,
+        (like((64, 1536), bf16), like((BLOCK, 1536), bf16)),
+        place,
+        velocity,
+        patch_pick.reshape(BLOCK, 1),
     )
     chosen_other = swap_cores(chosen)
     between, top = one_step(velocity, top, mine[0])
@@ -466,7 +507,14 @@
     between, top = lax.optimization_barrier((between, top, parts[3]))[:2]
     pieces = sum_plane(parts, place)
     wide = tuple(like((rows, LANES), f32) for rows in ROWS)
-    results = call(update_kernel, wide + wide + (like((16, BLOCK, LANES), bf16),), place, pieces, *layers, *moments)
+    results = call(
+        update_kernel,
+        wide + wide + (like((16, BLOCK, LANES), bf16),),
+        place,
+        pieces,
+        *layers,
+        *moments,
+    )
     mine, other = gather_matrices(exchange_planes(results[6]), place)
     current, _ = one_step(between, top, results[6])
     velocity_next = call(

time: 254 us -> 238 us (0.937)
  blocking collectives: 64.7 us -> 45.2 us
  starting transfers between devices: 54 us -> 66.3 us
  waiting for transfers between devices: 89.1 us -> 77.8 us
    ppermute x27 -> x21, waiting for transfers between devices: 76 us -> 46.5 us  [spread(): lax.ppermute(take(s), AXES, phase_pairs(phase, s))]
    ppermute x0 -> x8, waiting for transfers between devices: none -> 26.2 us  [shifted(): return lax.ppermute(array, AXES, phase_pairs(2, shift))]
    all_to_all x3 -> x2, blocking collectives: 64.7 us -> 45.2 us  [exchange_planes(): lax.all_to_all(blocks, AXES, 0, 0, tiled=True, axis_index_groups=planes())]
    ppermute x0 -> x8, starting transfers between devices: none -> 12.8 us  [shifted(): return lax.ppermute(array, AXES, phase_pairs(2, shift))]
    ppermute x27 -> x21, starting transfers between devices: 37.1 us -> 29.5 us  [spread(): lax.ppermute(take(s), AXES, phase_pairs(phase, s))]
    ppermute x4, waiting for transfers between devices: 5.08 us -> 0.01 us  [edges_of(): found.append(lax.ppermute(last, axis, up).astype(f32))]
    all_to_all x0 -> x1, starting transfers between devices: none -> 3.65 us  [exchange_planes(): lax.all_to_all(blocks, AXES, 0, 0, tiled=True, axis_index_groups=planes())]
    ppermute x10 -> x14, waiting for transfers between devices: 8.07 us -> 5.05 us  [swap_cores(): return lax.ppermute(array, 'role_1', [(0, 1), (1, 0)])]
  transfers between devices with their start and end apart: 45 -> 52, of which waited for: 24 -> 20; matrix products, arithmetic and copies ran while one was open for 0% -> 0% of each run, Pallas kernels for 8% -> 10%
where the time goes in v1:
time: 238 us; the launch traced here: 237 us
  waiting for transfers between devices  77.8 us (33%)
  starting transfers between devices  66.3 us (28%)
  blocking collectives  45.2 us (19%)
  Pallas kernels  40.8 us (17%)
  local copies, waits for them, and re-layouts  5.39 us (2%)
    ppermute x21, waiting for transfers between devices, spread(): lax.ppermute(take(s), AXES, phase_pairs(phase, s))  46.5 us
    all_to_all x2, blocking collectives, exchange_planes(): lax.all_to_all(blocks, AXES, 0, 0, tiled=True, axis_index_groups=planes())  45.2 us
    ppermute x21, starting transfers between devices, spread(): lax.ppermute(take(s), AXES, phase_pairs(phase, s))  29.5 us
    ppermute x8, waiting for transfers between devices, shifted(): return lax.ppermute(array, AXES, phase_pairs(2, shift))  26.2 us
    pallas_call x11, Pallas kernels, call(): pl.pallas_call(kernel, out_shape=outs, in_specs=[SMEM] + [VMEM] * len(arr...  23.2 us
    pallas_call x2, Pallas kernels, advect(): pl.pallas_call(advect_kernel, out_shape=(like(field.shape, f32), like((8,...  17 us
    ppermute x4, starting transfers between devices, edges_of(): lax.ppermute(leading, axis, [(b, a) for a, b in up]).astype(f32)  14.8 us
    ppermute x8, starting transfers between devices, shifted(): return lax.ppermute(array, AXES, phase_pairs(2, shift))  12.8 us
  transfers between devices with their start and end apart: 52, of which 20 were waited for; matrix products, arithmetic and copies ran while one was open for 0% of the time, Pallas kernels for 10%

profile of v1, /device:TPU:0, one launch (start us, length us, event | category | flops | bytes accessed | tf_op | source)
XLA Modules:
  0.0 236.8 jit_solution(1124925080279115772)
XLA Ops:
  4.1 25.3 %all_to_all.15.own = bf16[16,128,256]{2,1,0:T(8,128)(2,1)S(1)} all-to-all(bf16[16,128,256]{2,1,0:T(8,128)(2,1)S(1)} %own_block.1), channel_id=1, replica_groups={{0,4,64,68,8,12,72,76,16,20,80,84,24,28,88,92},{1,5,65,69,9,13,73,77,17..., dimensions={0} | all-to-all | bytes 2097152 | tf_op jit(solution)/shard_map/all_to_all | solution.py:54
  29.4 1.5 collective-permute-start.10
  30.9 1.8 collective-permute-start.11
  32.7 12.8 %collective-permute-done.10.one = bf16[16,128,256]{2,1,0:T(8,128)(2,1)S(1)} collective-permute-done((bf16[16,128,256]{2,1,0:T(8,128)(2,1)S(1)}, bf16[16,128,256]{2,1,0:T(8,128)(2,1)S(1)}, u32[]{:S(2)}, u32[]{:S(2)}) %collective-permute-start.10) | collective-permute-done | bytes 1048608 | tf_op jit(solution)/shard_map/ppermute | solution.py:150
  46.4 3.0 %collective-permute-start.13 = (bf16[8,128,256]{2,1,0:T(8,128)(2,1)S(1)}, bf16[8,128,256]{2,1,0:T(8,128)(2,1)}, u32[]{:S(2)}, u32[]{:S(2)}) collective-permute-start(bf16[8,128,256]{2,1,0:T(8,128)(2,1)S(1)} %slice.49), channel_id=1, source_target_pairs={{0,3},{1,0},{2,1},{3,2},{8,11},{9,8},{10,9},{11,10},{16,19},{17,16... | collective-permute-start | bytes 1572872 | tf_op jit(solution)/shard_map/ppermute | solution.py:150
  49.4 6.6 %collective-permute-done.12.low = bf16[8,128,256]{2,1,0:T(8,128)(2,1)} collective-permute-done((bf16[8,128,256]{2,1,0:T(8,128)(2,1)S(1)}, bf16[8,128,256]{2,1,0:T(8,128)(2,1)}, u32[]{:S(2)}, u32[]{:S(2)}) %collective-permute-start.12) | collective-permute-done | bytes 524320 | tf_op jit(solution)/shard_map/ppermute | solution.py:150
  58.2 2.1 shard_map.144
  61.0 1.7 shard_map.146
  62.7 2.7 %shard_map.148 = (bf16[2,1536,256]{2,1,0:T(8,128)(2,1)S(1)}, bf16[2,1024,256]{2,1,0:T(8,128)(2,1)S(1)}, bf16[2,1536,256]{2,1,0:T(8,128)(2,1)S(1)}) custom-call(s32[6]{0:T(128)S(1)} %stack.27.place, bf16[16,128,256]{2,1,0:T(8,128)(2,1)} %collective-permute-done.18.own, bf16[16,128,256]{2,1,0:T(8,128)(2,1)} %collective-permute-done.19.one, ...), custom_call_target="tpu_custom_call" | custom-call | tf_op jit(solution)/shard_map/pallas_call | solution.py:89
  65.4 4.5 %shard_map.149 = (bf16[128,4096]{1,0:T(8,128)(2,1)S(1)}, bf16[128,4096]{1,0:T(8,128)(2,1)S(1)}) custom-call(s32[6]{0:T(128)S(1)} %stack.27.place, bf16[128,1536]{1,0:T(8,128)(2,1)S(1)} %get-tuple-element.46.picked, bf16[128,1536]{1,0:T(8,128)(2,1)S(1)} %copy-done.7, bf16[2,1536,256]{2,1,0:T(8,128)(2,1)S(1)} %get-tuple-element.42.m1, ...), custom_call_target="tpu_custom_call" | custom-call | tf_op jit(solution)/shard_map/pallas_call | solution.py:89
  70.5 2.7 %collective-permute-done.24.picked_other = bf16[128,1536]{1,0:T(8,128)(2,1)S(1)} collective-permute-done((bf16[128,1536]{1,0:T(8,128)(2,1)S(1)}, bf16[128,1536]{1,0:T(8,128)(2,1)S(1)}, u32[]{:S(2)}, u32[]{:S(2)}) %collective-permute-start.24) | collective-permute-done | bytes 393248 | tf_op jit(solution)/shard_map/ppermute | solution.py:63
  73.2 2.1 shard_map.150
  76.1 2.9 %collective-permute-start.36 = (bf16[16,128,256]{2,1,0:T(8,128)(2,1)S(1)}, bf16[16,128,256]{2,1,0:T(8,128)(2,1)S(1)}, u32[]{:S(2)}, u32[]{:S(2)}) collective-permute-start(bf16[16,128,256]{2,1,0:T(8,128)(2,1)S(1)} %get-tuple-element.54), channel_id=1, source_target_pairs={{0,3},{1,0},{2,1},{3,2},{8,11},{9,8},{10,9},{11,10},{16,19},{17,16... | collective-permute-start | bytes 3145736 | tf_op jit(solution)/shard_map/ppermute | solution.py:59
  79.0 1.4 collective-permute-start.37
  80.4 11.3 %collective-permute-done.35.b = bf16[16,128,256]{2,1,0:T(8,128)(2,1)S(1)} collective-permute-done((bf16[16,128,256]{2,1,0:T(8,128)(2,1)S(1)}, bf16[16,128,256]{2,1,0:T(8,128)(2,1)S(1)}, u32[]{:S(2)}, u32[]{:S(2)}) %collective-permute-start.35) | collective-permute-done | bytes 1048608 | tf_op jit(solution)/shard_map/ppermute | solution.py:59
  91.7 10.9 %collective-permute-done.36.c = bf16[16,128,256]{2,1,0:T(8,128)(2,1)S(1)} collective-permute-done((bf16[16,128,256]{2,1,0:T(8,128)(2,1)S(1)}, bf16[16,128,256]{2,1,0:T(8,128)(2,1)S(1)}, u32[]{:S(2)}, u32[]{:S(2)}) %collective-permute-start.36) | collective-permute-done | bytes 1048608 | tf_op jit(solution)/shard_map/ppermute | solution.py:59
  102.5 1.8 collective-permute-done.37.d
  105.5 19.9 %all_to_all.16.pieces = bf16[16,128,256]{2,1,0:T(8,128)(2,1)S(1)} all-to-all(bf16[16,128,256]{2,1,0:T(8,128)(2,1)S(1)} %shard_map.151), channel_id=1, replica_groups={{0,4,64,68,8,12,72,76,16,20,80,84,24,28,88,92},{1,5,65,69,9,13,73,77,17..., dimensions={0} | all-to-all | bytes 2097152 | tf_op jit(solution)/shard_map/all_to_all | solution.py:54
  125.4 1.8 shard_map.152
  127.3 3.7 %all-to-all-start.2 = ((bf16[16,128,256]{2,1,0:T(8,128)(2,1)}), bf16[16,128,256]{2,1,0:T(8,128)(2,1)S(1)}, u32[]{:S(2)}, u32[]{:S(2)}) async-start(bf16[16,128,256]{2,1,0:T(8,128)(2,1)} %get-tuple-element.59), calls=%async_computation.2 | async-start | bytes 2097152 | tf_op jit(solution)/shard_map/all_to_all | solution.py:54
  133.3 3.3 %collective-permute-start.3 = (f32[8,128]{1,0:T(8,128)S(1)}, f32[8,128]{1,0:T(8,128)S(1)}, u32[]{:S(2)}, u32[]{:S(2)}) collective-permute-start(f32[8,128]{1,0:T(8,128)S(1)} %max.60), channel_id=1, source_target_pairs={{0,64},{1,65},{2,66},{3,67},{8,72},{9,73},{10,74},{11,75},{16,80},... | collective-permute-start | bytes 12296 | tf_op jit(solution)/shard_map/ppermute | solution.py:59
  138.6 6.7 %collective-permute-done.3 = f32[8,128]{1,0:T(8,128)S(1)} collective-permute-done((f32[8,128]{1,0:T(8,128)S(1)}, f32[8,128]{1,0:T(8,128)S(1)}, u32[]{:S(2)}, u32[]{:S(2)}) %collective-permute-start.3) | collective-permute-done | bytes 4128 | tf_op jit(solution)/shard_map/ppermute | solution.py:59
  145.4 1.2 collective-permute-start.6
  146.6 2.2 collective-permute-start.5
  149.3 3.2 %collective-permute-start.15 = (bf16[3,3,16,128]{3,2,1,0:T(8,128)(2,1)S(1)}, bf16[3,3,16,128]{3,2,1,0:T(8,128)(2,1)S(1)}, u32[]{:S(2)}, u32[]{:S(2)}) collective-permute-start(bf16[3,3,16,128]{3,2,1,0:T(8,128)(2,1)S(1)} %get-tuple-element.81), channel_id=1, source_target_pairs={{32,0},{64,32},{96,64},{0,96},{33,1},{65,33},{97,65},{1,97},{34,2}... | collective-permute-start | bytes 110600 | tf_op jit(solution)/shard_map/ppermute | solution.py:357
  153.6 2.6 %collective-permute-start.9 = (f32[8,128]{1,0:T(8,128)S(1)}, f32[8,128]{1,0:T(8,128)S(1)}, u32[]{:S(2)}, u32[]{:S(2)}) collective-permute-start(f32[8,128]{1,0:T(8,128)S(1)} %maximum_maximum_fusion.4), channel_id=1, source_target_pairs={{0,2},{1,3},{2,0},{3,1},{8,10},{9,11},{10,8},{11,9},{16,18},{17,19... | collective-permute-start | bytes 12296 | tf_op jit(solution)/shard_map/ppermute | solution.py:59
  156.2 1.5 collective-permute-start.8
  158.7 1.5 collective-permute-start.16
  160.2 4.8 %collective-permute-start.17 = (bf16[3,16,3,128]{3,2,1,0:T(4,128)(2,1)S(1)}, bf16[3,16,3,128]{3,2,1,0:T(4,128)(2,1)S(1)}, u32[]{:S(2)}, u32[]{:S(2)}) collective-permute-start(bf16[3,16,3,128]{3,2,1,0:T(4,128)(2,1)S(1)} %get-tuple-element.79), channel_id=1, source_target_pairs={{1,0},{2,1},{3,2},{4,3},{5,4},{6,5},{7,6},{8,7},{9,8},{10,9},{11,1... | collective-permute-start | bytes 110600 | tf_op jit(solution)/shard_map/ppermute | solution.py:357
  165.0 3.2 %collective-permute-start.43 = (bf16[16,128,256]{2,1,0:T(8,128)(2,1)S(1)}, bf16[16,128,256]{2,1,0:T(8,128)(2,1)S(1)}, u32[]{:S(2)}, u32[]{:S(2)}) collective-permute-start(bf16[16,128,256]{2,1,0:T(8,128)(2,1)S(1)} %all-to-all-done.2.own), channel_id=1, source_target_pairs={{0,3},{1,0},{2,1},{3,2},{8,11},{9,8},{10,9},{11,10},{16,19},{17,16... | collective-permute-start | bytes 3145736 | tf_op jit(solution)/shard_map/ppermute | solution.py:150
  168.3 8.2 %shard_map.147 = (f32[3,16,16,128]{3,2,1,0:T(8,128)S(1)}, f32[8,128]{1,0:T(8,128)S(1)}) custom-call(f32[8,128]{1,0:T(8,128)S(1)} %maximum_maximum_fusion.3.tops, f32[3,16,16,128]{3,2,1,0:T(8,128)S(1)} %copy-done, f32[3,3,16,128]{3,2,1,0:T(8,128)S(1)} %convert_element_type.31.low_x, f32[3,3,16,128]{3,2,1,0:T(8,128)S(1)} %convert_element_type.32.high_x, ...), custom_call_target="tpu_custom_call" | custom-call | tf_op jit(solution)/shard_map/pallas_call | solution.py:436
  177.7 1.3 collective-permute-start.28
  179.5 1.6 collective-permute-start.26
  181.1 1.8 collective-permute-done.28
  182.9 1.4 collective-permute-done.26
  184.3 1.4 collective-permute-start.31
  185.7 2.4 %collective-permute-start.30 = (f32[8,128]{1,0:T(8,128)S(1)}, f32[8,128]{1,0:T(8,128)S(1)}, u32[]{:S(2)}, u32[]{:S(2)}) collective-permute-start(f32[8,128]{1,0:T(8,128)S(1)} %maximum_maximum_fusion.2), channel_id=1, source_target_pairs={{0,24},{1,25},{2,26},{3,27},{8,0},{9,1},{10,2},{11,3},{16,8},{17,9... | collective-permute-start | bytes 12296 | tf_op jit(solution)/shard_map/ppermute | solution.py:59
  188.1 1.3 collective-permute-done.31
  189.4 3.5 %collective-permute-done.29 = f32[8,128]{1,0:T(8,128)S(1)} collective-permute-done((f32[8,128]{1,0:T(8,128)S(1)}, f32[8,128]{1,0:T(8,128)S(1)}, u32[]{:S(2)}, u32[]{:S(2)}) %collective-permute-start.29) | collective-permute-done | bytes 4128 | tf_op jit(solution)/shard_map/ppermute | solution.py:59
  192.9 3.5 %collective-permute-start.33 = (f32[8,128]{1,0:T(8,128)S(1)}, f32[8,128]{1,0:T(8,128)S(1)}, u32[]{:S(2)}, u32[]{:S(2)}) collective-permute-start(f32[8,128]{1,0:T(8,128)S(1)} %maximum_maximum_fusion.1), channel_id=1, source_target_pairs={{0,3},{1,0},{2,1},{3,2},{8,11},{9,8},{10,9},{11,10},{16,19},{17,16... | collective-permute-start | bytes 12296 | tf_op jit(solution)/shard_map/ppermute | solution.py:59
  196.4 1.6 collective-permute-done.34
  198.0 1.7 collective-permute-start.39
  200.8 5.1 %collective-permute-start.41 = (bf16[3,16,3,128]{3,2,1,0:T(4,128)(2,1)S(1)}, bf16[3,16,3,128]{3,2,1,0:T(4,128)(2,1)S(1)}, u32[]{:S(2)}, u32[]{:S(2)}) collective-permute-start(bf16[3,16,3,128]{3,2,1,0:T(4,128)(2,1)S(1)} %get-tuple-element.75), channel_id=1, source_target_pairs={{1,0},{2,1},{3,2},{4,3},{5,4},{6,5},{7,6},{8,7},{9,8},{10,9},{11,1... | collective-permute-start | bytes 110600 | tf_op jit(solution)/shard_map/ppermute | solution.py:357
  206.0 4.7 %collective-permute-done.32 = f32[8,128]{1,0:T(8,128)S(1)} collective-permute-done((f32[8,128]{1,0:T(8,128)S(1)}, f32[8,128]{1,0:T(8,128)S(1)}, u32[]{:S(2)}, u32[]{:S(2)}) %collective-permute-start.32) | collective-permute-done | bytes 4128 | tf_op jit(solution)/shard_map/ppermute | solution.py:59
  211.5 3.1 %collective-permute-start.45 = (bf16[8,128,256]{2,1,0:T(8,128)(2,1)S(1)}, bf16[8,128,256]{2,1,0:T(8,128)(2,1)S(1)}, u32[]{:S(2)}, u32[]{:S(2)}) collective-permute-start(bf16[8,128,256]{2,1,0:T(8,128)(2,1)S(1)} %slice.59), channel_id=1, source_target_pairs={{0,3},{1,0},{2,1},{3,2},{8,11},{9,8},{10,9},{11,10},{16,19},{17,16... | collective-permute-start | bytes 1572872 | tf_op jit(solution)/shard_map/ppermute | solution.py:150
  214.5 6.6 %collective-permute-done.44.low = bf16[8,128,256]{2,1,0:T(8,128)(2,1)S(1)} collective-permute-done((bf16[8,128,256]{2,1,0:T(8,128)(2,1)S(1)}, bf16[8,128,256]{2,1,0:T(8,128)(2,1)S(1)}, u32[]{:S(2)}, u32[]{:S(2)}) %collective-permute-start.44) | collective-permute-done | bytes 524320 | tf_op jit(solution)/shard_map/ppermute | solution.py:150
  221.7 8.8 %shard_map.153 = (f32[3,16,16,128]{3,2,1,0:T(8,128)S(1)}, f32[8,128]{1,0:T(8,128)}) custom-call(f32[8,128]{1,0:T(8,128)S(1)} %maximum_maximum_fusion.tops, f32[3,16,16,128]{3,2,1,0:T(8,128)S(1)} %get-tuple-element.61.field, f32[3,3,16,128]{3,2,1,0:T(8,128)S(1)} %convert_element_type.36.low_x, f32[3,3,16,128]{3,2,1,0:T(8,128)S(1)} %convert_element_type.37.high_x, ...), custom_call_target="tpu_custom_call" | custom-call | tf_op jit(solution)/shard_map/pallas_call | solution.py:436
  232.7 4.1 %shard_map.156 = f32[3,16,16,128]{3,2,1,0:T(8,128)} custom-call(s32[6]{0:T(128)S(1)} %stack.27.place, bf16[64,1536]{1,0:T(8,128)(2,1)S(1)} %copy-done.12, f32[3,16,16,128]{3,2,1,0:T(8,128)S(1)} %get-tuple-element.62.field, bf16[2,1536,256]{2,1,0:T(8,128)(2,1)S(1)} %get-tuple-element.63.m1, bf16[2,1024,256]{2,1,0:T(8,128)(2,1)S(1)} %get-tuple-element.64.m2, ...), custom_call_target="tpu_custom_call" | custom-call | tf_op jit(solution)/shard_map/pallas_call | solution.py:89
  (130 shorter events, 23.0 us)
Async XLA Ops:
  29.4 16.0 %collective-permute-start.10 = (bf16[16,128,256]{2,1,0:T(8,128)(2,1)S(1)}, bf16[16,128,256]{2,1,0:T(8,128)(2,1)S(1)}, u32[]{:S(2)}, u32[]{:S(2)}) collective-permute-start(bf16[16,128,256]{2,1,0:T(8,128)(2,1)S(1)} %all_to_all.15.own), channel_id=1, source_target_pairs={{0,1},{1,2},{2,3},{3,0},{8,9},{9,10},{10,11},{11,8},{16,17},{17,18... | collective-permute-start | bytes 3145736 | tf_op jit(solution)/shard_map/ppermute | solution.py:150
  30.9 14.9 %collective-permute-start.11 = (bf16[16,128,256]{2,1,0:T(8,128)(2,1)S(1)}, bf16[16,128,256]{2,1,0:T(8,128)(2,1)S(1)}, u32[]{:S(2)}, u32[]{:S(2)}) collective-permute-start(bf16[16,128,256]{2,1,0:T(8,128)(2,1)S(1)} %all_to_all.15.own), channel_id=1, source_target_pairs={{0,3},{1,0},{2,1},{3,2},{8,11},{9,8},{10,9},{11,10},{16,19},{17,16... | collective-permute-start | bytes 3145736 | tf_op jit(solution)/shard_map/ppermute | solution.py:150
  32.7 30.0 %collective-permute-start.18 = (bf16[16,128,256]{2,1,0:T(8,128)(2,1)S(1)}, bf16[16,128,256]{2,1,0:T(8,128)(2,1)}, u32[]{:S(2)}, u32[]{:S(2)}) collective-permute-start(bf16[16,128,256]{2,1,0:T(8,128)(2,1)S(1)} %all_to_all.15.own), channel_id=1, source_target_pairs={{0,32},{32,0},{1,33},{33,1},{2,34},{34,2},{3,35},{35,3},{4,36},{36... | collective-permute-start | bytes 3145736 | tf_op jit(solution)/shard_map/ppermute | solution.py:63
  45.5 10.6 %collective-permute-start.12 = (bf16[8,128,256]{2,1,0:T(8,128)(2,1)S(1)}, bf16[8,128,256]{2,1,0:T(8,128)(2,1)}, u32[]{:S(2)}, u32[]{:S(2)}) collective-permute-start(bf16[8,128,256]{2,1,0:T(8,128)(2,1)S(1)} %slice.48), channel_id=1, source_target_pairs={{0,1},{1,2},{2,3},{3,0},{8,9},{9,10},{10,11},{11,8},{16,17},{17,18... | collective-permute-start | bytes 1572872 | tf_op jit(solution)/shard_map/ppermute | solution.py:150
  45.8 16.9 %collective-permute-start.19 = (bf16[16,128,256]{2,1,0:T(8,128)(2,1)S(1)}, bf16[16,128,256]{2,1,0:T(8,128)(2,1)}, u32[]{:S(2)}, u32[]{:S(2)}) collective-permute-start(bf16[16,128,256]{2,1,0:T(8,128)(2,1)S(1)} %collective-permute-done.10.one), channel_id=1, source_target_pairs={{0,32},{32,0},{1,33},{33,1},{2,34},{34,2},{3,35},{35,3},{4,36},{36... | collective-permute-start | bytes 3145736 | tf_op jit(solution)/shard_map/ppermute | solution.py:63
  45.9 16.9 %collective-permute-start.20 = (bf16[16,128,256]{2,1,0:T(8,128)(2,1)S(1)}, bf16[16,128,256]{2,1,0:T(8,128)(2,1)}, u32[]{:S(2)}, u32[]{:S(2)}) collective-permute-start(bf16[16,128,256]{2,1,0:T(8,128)(2,1)S(1)} %collective-permute-done.11.three), channel_id=1, source_target_pairs={{0,32},{32,0},{1,33},{33,1},{2,34},{34,2},{3,35},{35,3},{4,36},{36... | collective-permute-start | bytes 3145736 | tf_op jit(solution)/shard_map/ppermute | solution.py:63
  46.4 9.7 %collective-permute-start.13 = (bf16[8,128,256]{2,1,0:T(8,128)(2,1)S(1)}, bf16[8,128,256]{2,1,0:T(8,128)(2,1)}, u32[]{:S(2)}, u32[]{:S(2)}) collective-permute-start(bf16[8,128,256]{2,1,0:T(8,128)(2,1)S(1)} %slice.49), channel_id=1, source_target_pairs={{0,3},{1,0},{2,1},{3,2},{8,11},{9,8},{10,9},{11,10},{16,19},{17,16... | collective-permute-start | bytes 1572872 | tf_op jit(solution)/shard_map/ppermute | solution.py:150
  56.1 6.7 %collective-permute-start.21 = (bf16[8,128,256]{2,1,0:T(8,128)(2,1)}, bf16[8,128,256]{2,1,0:T(8,128)(2,1)}, u32[]{:S(2)}, u32[]{:S(2)}) collective-permute-start(bf16[8,128,256]{2,1,0:T(8,128)(2,1)} %collective-permute-done.12.low), channel_id=1, source_target_pairs={{0,32},{32,0},{1,33},{33,1},{2,34},{34,2},{3,35},{35,3},{4,36},{36... | collective-permute-start | bytes 1572872 | tf_op jit(solution)/shard_map/ppermute | solution.py:63
  56.1 6.6 %collective-permute-start.22 = (bf16[8,128,256]{2,1,0:T(8,128)(2,1)}, bf16[8,128,256]{2,1,0:T(8,128)(2,1)}, u32[]{:S(2)}, u32[]{:S(2)}) collective-permute-start(bf16[8,128,256]{2,1,0:T(8,128)(2,1)} %collective-permute-done.13.high_part), channel_id=1, source_target_pairs={{0,32},{32,0},{1,33},{33,1},{2,34},{34,2},{3,35},{35,3},{4,36},{36... | collective-permute-start | bytes 1572872 | tf_op jit(solution)/shard_map/ppermute | solution.py:63
  75.3 16.4 %collective-permute-start.35 = (bf16[16,128,256]{2,1,0:T(8,128)(2,1)S(1)}, bf16[16,128,256]{2,1,0:T(8,128)(2,1)S(1)}, u32[]{:S(2)}, u32[]{:S(2)}) collective-permute-start(bf16[16,128,256]{2,1,0:T(8,128)(2,1)S(1)} %get-tuple-element.57), channel_id=1, source_target_pairs={{0,1},{1,2},{2,3},{3,0},{8,9},{9,10},{10,11},{11,8},{16,17},{17,18... | collective-permute-start | bytes 3145736 | tf_op jit(solution)/shard_map/ppermute | solution.py:59
  76.1 26.4 %collective-permute-start.36 = (bf16[16,128,256]{2,1,0:T(8,128)(2,1)S(1)}, bf16[16,128,256]{2,1,0:T(8,128)(2,1)S(1)}, u32[]{:S(2)}, u32[]{:S(2)}) collective-permute-start(bf16[16,128,256]{2,1,0:T(8,128)(2,1)S(1)} %get-tuple-element.54), channel_id=1, source_target_pairs={{0,3},{1,0},{2,1},{3,2},{8,11},{9,8},{10,9},{11,10},{16,19},{17,16... | collective-permute-start | bytes 3145736 | tf_op jit(solution)/shard_map/ppermute | solution.py:59
  79.0 25.4 %collective-permute-start.37 = (bf16[16,128,256]{2,1,0:T(8,128)(2,1)S(1)}, bf16[16,128,256]{2,1,0:T(8,128)(2,1)S(1)}, u32[]{:S(2)}, u32[]{:S(2)}) collective-permute-start(bf16[16,128,256]{2,1,0:T(8,128)(2,1)S(1)} %get-tuple-element.58), channel_id=1, source_target_pairs={{0,2},{1,3},{2,0},{3,1},{8,10},{9,11},{10,8},{11,9},{16,18},{17,19... | collective-permute-start | bytes 3145736 | tf_op jit(solution)/shard_map/ppermute | solution.py:59
  127.3 37.7 %all-to-all-start.2 = ((bf16[16,128,256]{2,1,0:T(8,128)(2,1)}), bf16[16,128,256]{2,1,0:T(8,128)(2,1)S(1)}, u32[]{:S(2)}, u32[]{:S(2)}) async-start(bf16[16,128,256]{2,1,0:T(8,128)(2,1)} %get-tuple-element.59), calls=%async_computation.2 | async-start | bytes 2097152 | tf_op jit(solution)/shard_map/all_to_all | solution.py:54
  133.3 12.1 %collective-permute-start.3 = (f32[8,128]{1,0:T(8,128)S(1)}, f32[8,128]{1,0:T(8,128)S(1)}, u32[]{:S(2)}, u32[]{:S(2)}) collective-permute-start(f32[8,128]{1,0:T(8,128)S(1)} %max.60), channel_id=1, source_target_pairs={{0,64},{1,65},{2,66},{3,67},{8,72},{9,73},{10,74},{11,75},{16,80},... | collective-permute-start | bytes 12296 | tf_op jit(solution)/shard_map/ppermute | solution.py:59
  136.6 8.8 %collective-permute-start.2 = (f32[8,128]{1,0:T(8,128)S(1)}, f32[8,128]{1,0:T(8,128)S(1)}, u32[]{:S(2)}, u32[]{:S(2)}) collective-permute-start(f32[8,128]{1,0:T(8,128)S(1)} %max.60), channel_id=1, source_target_pairs={{0,68},{1,69},{2,70},{3,71},{8,76},{9,77},{10,78},{11,79},{16,84},... | collective-permute-start | bytes 12296 | tf_op jit(solution)/shard_map/ppermute | solution.py:59
  137.8 7.6 %collective-permute-start.1 = (f32[8,128]{1,0:T(8,128)S(1)}, f32[8,128]{1,0:T(8,128)S(1)}, u32[]{:S(2)}, u32[]{:S(2)}) collective-permute-start(f32[8,128]{1,0:T(8,128)S(1)} %max.60), channel_id=1, source_target_pairs={{0,4},{1,5},{2,6},{3,7},{8,12},{9,13},{10,14},{11,15},{16,20},{17,... | collective-permute-start | bytes 12296 | tf_op jit(solution)/shard_map/ppermute | solution.py:59
  145.4 7.1 %collective-permute-start.6 = (f32[8,128]{1,0:T(8,128)S(1)}, f32[8,128]{1,0:T(8,128)S(1)}, u32[]{:S(2)}, u32[]{:S(2)}) collective-permute-start(f32[8,128]{1,0:T(8,128)S(1)} %maximum_maximum_fusion.5), channel_id=1, source_target_pairs={{0,16},{1,17},{2,18},{3,19},{8,24},{9,25},{10,26},{11,27},{16,0},{... | collective-permute-start | bytes 12296 | tf_op jit(solution)/shard_map/ppermute | solution.py:59
  146.6 5.9 %collective-permute-start.5 = (f32[8,128]{1,0:T(8,128)S(1)}, f32[8,128]{1,0:T(8,128)S(1)}, u32[]{:S(2)}, u32[]{:S(2)}) collective-permute-start(f32[8,128]{1,0:T(8,128)S(1)} %maximum_maximum_fusion.5), channel_id=1, source_target_pairs={{0,24},{1,25},{2,26},{3,27},{8,0},{9,1},{10,2},{11,3},{16,8},{17,9... | collective-permute-start | bytes 12296 | tf_op jit(solution)/shard_map/ppermute | solution.py:59
  148.8 4.8 %collective-permute-start.4 = (f32[8,128]{1,0:T(8,128)S(1)}, f32[8,128]{1,0:T(8,128)S(1)}, u32[]{:S(2)}, u32[]{:S(2)}) collective-permute-start(f32[8,128]{1,0:T(8,128)S(1)} %maximum_maximum_fusion.5), channel_id=1, source_target_pairs={{0,8},{1,9},{2,10},{3,11},{8,16},{9,17},{10,18},{11,19},{16,24},{1... | collective-permute-start | bytes 12296 | tf_op jit(solution)/shard_map/ppermute | solution.py:59
  149.3 15.7 %collective-permute-start.14 = (bf16[3,3,16,128]{3,2,1,0:T(8,128)(2,1)S(1)}, bf16[3,3,16,128]{3,2,1,0:T(8,128)(2,1)S(1)}, u32[]{:S(2)}, u32[]{:S(2)}) collective-permute-start(bf16[3,3,16,128]{3,2,1,0:T(8,128)(2,1)S(1)} %get-tuple-element.82), channel_id=1, source_target_pairs={{0,32},{32,64},{64,96},{96,0},{1,33},{33,65},{65,97},{97,1},{2,34}... | collective-permute-start | bytes 110600 | tf_op jit(solution)/shard_map/ppermute | solution.py:356
  149.3 18.9 %collective-permute-start.15 = (bf16[3,3,16,128]{3,2,1,0:T(8,128)(2,1)S(1)}, bf16[3,3,16,128]{3,2,1,0:T(8,128)(2,1)S(1)}, u32[]{:S(2)}, u32[]{:S(2)}) collective-permute-start(bf16[3,3,16,128]{3,2,1,0:T(8,128)(2,1)S(1)} %get-tuple-element.81), channel_id=1, source_target_pairs={{32,0},{64,32},{96,64},{0,96},{33,1},{65,33},{97,65},{1,97},{34,2}... | collective-permute-start | bytes 110600 | tf_op jit(solution)/shard_map/ppermute | solution.py:357
  153.6 5.1 %collective-permute-start.9 = (f32[8,128]{1,0:T(8,128)S(1)}, f32[8,128]{1,0:T(8,128)S(1)}, u32[]{:S(2)}, u32[]{:S(2)}) collective-permute-start(f32[8,128]{1,0:T(8,128)S(1)} %maximum_maximum_fusion.4), channel_id=1, source_target_pairs={{0,2},{1,3},{2,0},{3,1},{8,10},{9,11},{10,8},{11,9},{16,18},{17,19... | collective-permute-start | bytes 12296 | tf_op jit(solution)/shard_map/ppermute | solution.py:59
  156.2 4.0 %collective-permute-start.8 = (f32[8,128]{1,0:T(8,128)S(1)}, f32[8,128]{1,0:T(8,128)S(1)}, u32[]{:S(2)}, u32[]{:S(2)}) collective-permute-start(f32[8,128]{1,0:T(8,128)S(1)} %maximum_maximum_fusion.4), channel_id=1, source_target_pairs={{0,3},{1,0},{2,1},{3,2},{8,11},{9,8},{10,9},{11,10},{16,19},{17,16... | collective-permute-start | bytes 12296 | tf_op jit(solution)/shard_map/ppermute | solution.py:59
  157.8 7.2 %collective-permute-start.7 = (f32[8,128]{1,0:T(8,128)S(1)}, f32[8,128]{1,0:T(8,128)S(1)}, u32[]{:S(2)}, u32[]{:S(2)}) collective-permute-start(f32[8,128]{1,0:T(8,128)S(1)} %maximum_maximum_fusion.4), channel_id=1, source_target_pairs={{0,1},{1,2},{2,3},{3,0},{8,9},{9,10},{10,11},{11,8},{16,17},{17,18... | collective-permute-start | bytes 12296 | tf_op jit(solution)/shard_map/ppermute | solution.py:59
  158.7 9.5 %collective-permute-start.16 = (bf16[3,16,3,128]{3,2,1,0:T(4,128)(2,1)S(1)}, bf16[3,16,3,128]{3,2,1,0:T(4,128)(2,1)S(1)}, u32[]{:S(2)}, u32[]{:S(2)}) collective-permute-start(bf16[3,16,3,128]{3,2,1,0:T(4,128)(2,1)S(1)} %get-tuple-element.80), channel_id=1, source_target_pairs={{0,1},{1,2},{2,3},{3,4},{4,5},{5,6},{6,7},{7,8},{8,9},{9,10},{10,1... | collective-permute-start | bytes 110600 | tf_op jit(solution)/shard_map/ppermute | solution.py:356
  160.2 8.1 %collective-permute-start.17 = (bf16[3,16,3,128]{3,2,1,0:T(4,128)(2,1)S(1)}, bf16[3,16,3,128]{3,2,1,0:T(4,128)(2,1)S(1)}, u32[]{:S(2)}, u32[]{:S(2)}) collective-permute-start(bf16[3,16,3,128]{3,2,1,0:T(4,128)(2,1)S(1)} %get-tuple-element.79), channel_id=1, source_target_pairs={{1,0},{2,1},{3,2},{4,3},{5,4},{6,5},{7,6},{8,7},{9,8},{10,9},{11,1... | collective-permute-start | bytes 110600 | tf_op jit(solution)/shard_map/ppermute | solution.py:357
  165.0 35.8 %collective-permute-start.42 = (bf16[16,128,256]{2,1,0:T(8,128)(2,1)S(1)}, bf16[16,128,256]{2,1,0:T(8,128)(2,1)S(1)}, u32[]{:S(2)}, u32[]{:S(2)}) collective-permute-start(bf16[16,128,256]{2,1,0:T(8,128)(2,1)S(1)} %all-to-all-done.2.own), channel_id=1, source_target_pairs={{0,1},{1,2},{2,3},{3,0},{8,9},{9,10},{10,11},{11,8},{16,17},{17,18... | collective-permute-start | bytes 3145736 | tf_op jit(solution)/shard_map/ppermute | solution.py:150
  165.0 40.9 %collective-permute-start.43 = (bf16[16,128,256]{2,1,0:T(8,128)(2,1)S(1)}, bf16[16,128,256]{2,1,0:T(8,128)(2,1)S(1)}, u32[]{:S(2)}, u32[]{:S(2)}) collective-permute-start(bf16[16,128,256]{2,1,0:T(8,128)(2,1)S(1)} %all-to-all-done.2.own), channel_id=1, source_target_pairs={{0,3},{1,0},{2,1},{3,2},{8,11},{9,8},{10,9},{11,10},{16,19},{17,16... | collective-permute-start | bytes 3145736 | tf_op jit(solution)/shard_map/ppermute | solution.py:150
  177.7 5.1 %collective-permute-start.28 = (f32[8,128]{1,0:T(8,128)S(1)}, f32[8,128]{1,0:T(8,128)S(1)}, u32[]{:S(2)}, u32[]{:S(2)}) collective-permute-start(f32[8,128]{1,0:T(8,128)S(1)} %max.70), channel_id=1, source_target_pairs={{0,64},{1,65},{2,66},{3,67},{8,72},{9,73},{10,74},{11,75},{16,80},... | collective-permute-start | bytes 12296 | tf_op jit(solution)/shard_map/ppermute | solution.py:59
  179.0 3.8 %collective-permute-start.27 = (f32[8,128]{1,0:T(8,128)S(1)}, f32[8,128]{1,0:T(8,128)S(1)}, u32[]{:S(2)}, u32[]{:S(2)}) collective-permute-start(f32[8,128]{1,0:T(8,128)S(1)} %max.70), channel_id=1, source_target_pairs={{0,68},{1,69},{2,70},{3,71},{8,76},{9,77},{10,78},{11,79},{16,84},... | collective-permute-start | bytes 12296 | tf_op jit(solution)/shard_map/ppermute | solution.py:59
  179.5 4.8 %collective-permute-start.26 = (f32[8,128]{1,0:T(8,128)S(1)}, f32[8,128]{1,0:T(8,128)S(1)}, u32[]{:S(2)}, u32[]{:S(2)}) collective-permute-start(f32[8,128]{1,0:T(8,128)S(1)} %max.70), channel_id=1, source_target_pairs={{0,4},{1,5},{2,6},{3,7},{8,12},{9,13},{10,14},{11,15},{16,20},{17,... | collective-permute-start | bytes 12296 | tf_op jit(solution)/shard_map/ppermute | solution.py:59
  184.3 5.1 %collective-permute-start.31 = (f32[8,128]{1,0:T(8,128)S(1)}, f32[8,128]{1,0:T(8,128)S(1)}, u32[]{:S(2)}, u32[]{:S(2)}) collective-permute-start(f32[8,128]{1,0:T(8,128)S(1)} %maximum_maximum_fusion.2), channel_id=1, source_target_pairs={{0,16},{1,17},{2,18},{3,19},{8,24},{9,25},{10,26},{11,27},{16,0},{... | collective-permute-start | bytes 12296 | tf_op jit(solution)/shard_map/ppermute | solution.py:59
  185.7 3.7 %collective-permute-start.30 = (f32[8,128]{1,0:T(8,128)S(1)}, f32[8,128]{1,0:T(8,128)S(1)}, u32[]{:S(2)}, u32[]{:S(2)}) collective-permute-start(f32[8,128]{1,0:T(8,128)S(1)} %maximum_maximum_fusion.2), channel_id=1, source_target_pairs={{0,24},{1,25},{2,26},{3,27},{8,0},{9,1},{10,2},{11,3},{16,8},{17,9... | collective-permute-start | bytes 12296 | tf_op jit(solution)/shard_map/ppermute | solution.py:59
  188.1 4.8 %collective-permute-start.29 = (f32[8,128]{1,0:T(8,128)S(1)}, f32[8,128]{1,0:T(8,128)S(1)}, u32[]{:S(2)}, u32[]{:S(2)}) collective-permute-start(f32[8,128]{1,0:T(8,128)S(1)} %maximum_maximum_fusion.2), channel_id=1, source_target_pairs={{0,8},{1,9},{2,10},{3,11},{8,16},{9,17},{10,18},{11,19},{16,24},{1... | collective-permute-start | bytes 12296 | tf_op jit(solution)/shard_map/ppermute | solution.py:59
  192.9 5.1 %collective-permute-start.34 = (f32[8,128]{1,0:T(8,128)S(1)}, f32[8,128]{1,0:T(8,128)S(1)}, u32[]{:S(2)}, u32[]{:S(2)}) collective-permute-start(f32[8,128]{1,0:T(8,128)S(1)} %maximum_maximum_fusion.1), channel_id=1, source_target_pairs={{0,2},{1,3},{2,0},{3,1},{8,10},{9,11},{10,8},{11,9},{16,18},{17,19... | collective-permute-start | bytes 12296 | tf_op jit(solution)/shard_map/ppermute | solution.py:59
  192.9 6.8 %collective-permute-start.33 = (f32[8,128]{1,0:T(8,128)S(1)}, f32[8,128]{1,0:T(8,128)S(1)}, u32[]{:S(2)}, u32[]{:S(2)}) collective-permute-start(f32[8,128]{1,0:T(8,128)S(1)} %maximum_maximum_fusion.1), channel_id=1, source_target_pairs={{0,3},{1,0},{2,1},{3,2},{8,11},{9,8},{10,9},{11,10},{16,19},{17,16... | collective-permute-start | bytes 12296 | tf_op jit(solution)/shard_map/ppermute | solution.py:59
  196.4 14.3 %collective-permute-start.38 = (bf16[3,3,16,128]{3,2,1,0:T(8,128)(2,1)S(1)}, bf16[3,3,16,128]{3,2,1,0:T(8,128)(2,1)S(1)}, u32[]{:S(2)}, u32[]{:S(2)}) collective-permute-start(bf16[3,3,16,128]{3,2,1,0:T(8,128)(2,1)S(1)} %get-tuple-element.78), channel_id=1, source_target_pairs={{0,32},{32,64},{64,96},{96,0},{1,33},{33,65},{65,97},{97,1},{2,34}... | collective-permute-start | bytes 110600 | tf_op jit(solution)/shard_map/ppermute | solution.py:356
  198.0 12.8 %collective-permute-start.39 = (bf16[3,3,16,128]{3,2,1,0:T(8,128)(2,1)S(1)}, bf16[3,3,16,128]{3,2,1,0:T(8,128)(2,1)S(1)}, u32[]{:S(2)}, u32[]{:S(2)}) collective-permute-start(bf16[3,3,16,128]{3,2,1,0:T(8,128)(2,1)S(1)} %get-tuple-element.77), channel_id=1, source_target_pairs={{32,0},{64,32},{96,64},{0,96},{33,1},{65,33},{97,65},{1,97},{34,2}... | collective-permute-start | bytes 110600 | tf_op jit(solution)/shard_map/ppermute | solution.py:357
  199.7 11.7 %collective-permute-start.40 = (bf16[3,16,3,128]{3,2,1,0:T(4,128)(2,1)S(1)}, bf16[3,16,3,128]{3,2,1,0:T(4,128)(2,1)S(1)}, u32[]{:S(2)}, u32[]{:S(2)}) collective-permute-start(bf16[3,16,3,128]{3,2,1,0:T(4,128)(2,1)S(1)} %get-tuple-element.76), channel_id=1, source_target_pairs={{0,1},{1,2},{2,3},{3,4},{4,5},{5,6},{6,7},{7,8},{8,9},{9,10},{10,1... | collective-permute-start | bytes 110600 | tf_op jit(solution)/shard_map/ppermute | solution.py:356
  200.8 10.7 %collective-permute-start.41 = (bf16[3,16,3,128]{3,2,1,0:T(4,128)(2,1)S(1)}, bf16[3,16,3,128]{3,2,1,0:T(4,128)(2,1)S(1)}, u32[]{:S(2)}, u32[]{:S(2)}) collective-permute-start(bf16[3,16,3,128]{3,2,1,0:T(4,128)(2,1)S(1)} %get-tuple-element.75), channel_id=1, source_target_pairs={{1,0},{2,1},{3,2},{4,3},{5,4},{6,5},{7,6},{8,7},{9,8},{10,9},{11,1... | collective-permute-start | bytes 110600 | tf_op jit(solution)/shard_map/ppermute | solution.py:357
  205.9 4.8 %collective-permute-start.32 = (f32[8,128]{1,0:T(8,128)S(1)}, f32[8,128]{1,0:T(8,128)S(1)}, u32[]{:S(2)}, u32[]{:S(2)}) collective-permute-start(f32[8,128]{1,0:T(8,128)S(1)} %maximum_maximum_fusion.1), channel_id=1, source_target_pairs={{0,1},{1,2},{2,3},{3,0},{8,9},{9,10},{10,11},{11,8},{16,17},{17,18... | collective-permute-start | bytes 12296 | tf_op jit(solution)/shard_map/ppermute | solution.py:59
  210.8 20.8 %collective-permute-start.46 = (bf16[16,128,256]{2,1,0:T(8,128)(2,1)S(1)}, bf16[16,128,256]{2,1,0:T(8,128)(2,1)S(1)}, u32[]{:S(2)}, u32[]{:S(2)}) collective-permute-start(bf16[16,128,256]{2,1,0:T(8,128)(2,1)S(1)} %all-to-all-done.2.own), channel_id=1, source_target_pairs={{0,32},{32,0},{1,33},{33,1},{2,34},{34,2},{3,35},{35,3},{4,36},{36... | collective-permute-start | bytes 3145736 | tf_op jit(solution)/shard_map/ppermute | solution.py:63
  210.8 10.4 %collective-permute-start.44 = (bf16[8,128,256]{2,1,0:T(8,128)(2,1)S(1)}, bf16[8,128,256]{2,1,0:T(8,128)(2,1)S(1)}, u32[]{:S(2)}, u32[]{:S(2)}) collective-permute-start(bf16[8,128,256]{2,1,0:T(8,128)(2,1)S(1)} %slice.58), channel_id=1, source_target_pairs={{0,1},{1,2},{2,3},{3,0},{8,9},{9,10},{10,11},{11,8},{16,17},{17,18... | collective-permute-start | bytes 1572872 | tf_op jit(solution)/shard_map/ppermute | solution.py:150
  210.8 20.8 %collective-permute-start.47 = (bf16[16,128,256]{2,1,0:T(8,128)(2,1)S(1)}, bf16[16,128,256]{2,1,0:T(8,128)(2,1)S(1)}, u32[]{:S(2)}, u32[]{:S(2)}) collective-permute-start(bf16[16,128,256]{2,1,0:T(8,128)(2,1)S(1)} %collective-permute-done.42.one), channel_id=1, source_target_pairs={{0,32},{32,0},{1,33},{33,1},{2,34},{34,2},{3,35},{35,3},{4,36},{36... | collective-permute-start | bytes 3145736 | tf_op jit(solution)/shard_map/ppermute | solution.py:63
  211.4 20.2 %collective-permute-start.48 = (bf16[16,128,256]{2,1,0:T(8,128)(2,1)S(1)}, bf16[16,128,256]{2,1,0:T(8,128)(2,1)S(1)}, u32[]{:S(2)}, u32[]{:S(2)}) collective-permute-start(bf16[16,128,256]{2,1,0:T(8,128)(2,1)S(1)} %collective-permute-done.43.three), channel_id=1, source_target_pairs={{0,32},{32,0},{1,33},{33,1},{2,34},{34,2},{3,35},{35,3},{4,36},{36... | collective-permute-start | bytes 3145736 | tf_op jit(solution)/shard_map/ppermute | solution.py:63
  211.5 9.8 %collective-permute-start.45 = (bf16[8,128,256]{2,1,0:T(8,128)(2,1)S(1)}, bf16[8,128,256]{2,1,0:T(8,128)(2,1)S(1)}, u32[]{:S(2)}, u32[]{:S(2)}) collective-permute-start(bf16[8,128,256]{2,1,0:T(8,128)(2,1)S(1)} %slice.59), channel_id=1, source_target_pairs={{0,3},{1,0},{2,1},{3,2},{8,11},{9,8},{10,9},{11,10},{16,19},{17,16... | collective-permute-start | bytes 1572872 | tf_op jit(solution)/shard_map/ppermute | solution.py:150
  221.2 10.4 %collective-permute-start.49 = (bf16[8,128,256]{2,1,0:T(8,128)(2,1)S(1)}, bf16[8,128,256]{2,1,0:T(8,128)(2,1)S(1)}, u32[]{:S(2)}, u32[]{:S(2)}) collective-permute-start(bf16[8,128,256]{2,1,0:T(8,128)(2,1)S(1)} %collective-permute-done.44.low), channel_id=1, source_target_pairs={{0,32},{32,0},{1,33},{33,1},{2,34},{34,2},{3,35},{35,3},{4,36},{36... | collective-permute-start | bytes 1572872 | tf_op jit(solution)/shard_map/ppermute | solution.py:63
  221.2 10.4 %collective-permute-start.50 = (bf16[8,128,256]{2,1,0:T(8,128)(2,1)S(1)}, bf16[8,128,256]{2,1,0:T(8,128)(2,1)S(1)}, u32[]{:S(2)}, u32[]{:S(2)}) collective-permute-start(bf16[8,128,256]{2,1,0:T(8,128)(2,1)S(1)} %collective-permute-done.45.high_part), channel_id=1, source_target_pairs={{0,32},{32,0},{1,33},{33,1},{2,34},{34,2},{3,35},{35,3},{4,36},{36... | collective-permute-start | bytes 1572872 | tf_op jit(solution)/shard_map/ppermute | solution.py:63
  (19 other events, 191.8 us)

commit v2 on v1

--- a/solution.py
+++ b/solution.py
@@ -353,8 +353,8 @@
         up = [(i, (i + 1) % size) for i in range(size)]
         last = lax.slice_in_dim(rounded, length - 3, length, axis=dim)
         leading = lax.slice_in_dim(rounded, 0, 3, axis=dim)
-        found.append(lax.ppermute(last, axis, up).astype(f32))
-        found.append(lax.ppermute(leading, axis, [(b, a) for a, b in up]).astype(f32))
+        found.append(lax.ppermute(last, axis, up))
+        found.append(lax.ppermute(leading, axis, [(b, a) for a, b in up]))
     return found
 
 
@@ -460,6 +460,7 @@
 def one_step(current, top, first):
     tops = after(global_tops(top), first)
     edges = edges_of(current)
+    edges = [edge.astype(f32) for edge in edges]
     return advect(tops, current, edges)
 
 

time: 238 us -> 238 us (level)
  no operation moved by 1% of the time
where the time goes in v2:
time: 238 us; the launch traced here: 237 us
  waiting for transfers between devices  77.8 us (33%)
  starting transfers between devices  66.3 us (28%)
  blocking collectives  45.2 us (19%)
  Pallas kernels  40.8 us (17%)
  local copies, waits for them, and re-layouts  5.39 us (2%)
    ppermute x21, waiting for transfers between devices, spread(): lax.ppermute(take(s), AXES, phase_pairs(phase, s))  46.5 us
    all_to_all x2, blocking collectives, exchange_planes(): lax.all_to_all(blocks, AXES, 0, 0, tiled=True, axis_index_groups=planes())  45.2 us
    ppermute x21, starting transfers between devices, spread(): lax.ppermute(take(s), AXES, phase_pairs(phase, s))  29.5 us
    ppermute x8, waiting for transfers between devices, shifted(): return lax.ppermute(array, AXES, phase_pairs(2, shift))  26.2 us
    pallas_call x11, Pallas kernels, call(): pl.pallas_call(kernel, out_shape=outs, in_specs=[SMEM] + [VMEM] * len(arr...  23.2 us
    pallas_call x2, Pallas kernels, advect(): pl.pallas_call(advect_kernel, out_shape=(like(field.shape, f32), like((8,...  17 us
    ppermute x4, starting transfers between devices, edges_of(): found.append(lax.ppermute(leading, axis, [(b, a) for a, b in up]))  14.8 us
    ppermute x8, starting transfers between devices, shifted(): return lax.ppermute(array, AXES, phase_pairs(2, shift))  12.8 us
  transfers between devices with their start and end apart: 52, of which 20 were waited for; matrix products, arithmetic and copies ran while one was open for 0% of the time, Pallas kernels for 10%

profile of v2, /device:TPU:0, one launch (start us, length us, event | category | flops | bytes accessed | tf_op | source)
XLA Modules:
  0.0 236.8 jit_solution(1124925080279115772)
XLA Ops:
  4.1 25.3 %all_to_all.15.own = bf16[16,128,256]{2,1,0:T(8,128)(2,1)S(1)} all-to-all(bf16[16,128,256]{2,1,0:T(8,128)(2,1)S(1)} %own_block.1), channel_id=1, replica_groups={{0,4,64,68,8,12,72,76,16,20,80,84,24,28,88,92},{1,5,65,69,9,13,73,77,17..., dimensions={0} | all-to-all | bytes 2097152 | tf_op jit(solution)/shard_map/all_to_all | solution.py:54
  29.4 1.5 collective-permute-start.10
  30.9 1.8 collective-permute-start.11
  32.7 12.8 %collective-permute-done.10.one = bf16[16,128,256]{2,1,0:T(8,128)(2,1)S(1)} collective-permute-done((bf16[16,128,256]{2,1,0:T(8,128)(2,1)S(1)}, bf16[16,128,256]{2,1,0:T(8,128)(2,1)S(1)}, u32[]{:S(2)}, u32[]{:S(2)}) %collective-permute-start.10) | collective-permute-done | bytes 1048608 | tf_op jit(solution)/shard_map/ppermute | solution.py:150
  46.4 3.0 %collective-permute-start.13 = (bf16[8,128,256]{2,1,0:T(8,128)(2,1)S(1)}, bf16[8,128,256]{2,1,0:T(8,128)(2,1)}, u32[]{:S(2)}, u32[]{:S(2)}) collective-permute-start(bf16[8,128,256]{2,1,0:T(8,128)(2,1)S(1)} %slice.49), channel_id=1, source_target_pairs={{0,3},{1,0},{2,1},{3,2},{8,11},{9,8},{10,9},{11,10},{16,19},{17,16... | collective-permute-start | bytes 1572872 | tf_op jit(solution)/shard_map/ppermute | solution.py:150
  49.4 6.6 %collective-permute-done.12.low = bf16[8,128,256]{2,1,0:T(8,128)(2,1)} collective-permute-done((bf16[8,128,256]{2,1,0:T(8,128)(2,1)S(1)}, bf16[8,128,256]{2,1,0:T(8,128)(2,1)}, u32[]{:S(2)}, u32[]{:S(2)}) %collective-permute-start.12) | collective-permute-done | bytes 524320 | tf_op jit(solution)/shard_map/ppermute | solution.py:150
  58.2 2.1 shard_map.144
  61.0 1.7 shard_map.146
  62.7 2.7 %shard_map.148 = (bf16[2,1536,256]{2,1,0:T(8,128)(2,1)S(1)}, bf16[2,1024,256]{2,1,0:T(8,128)(2,1)S(1)}, bf16[2,1536,256]{2,1,0:T(8,128)(2,1)S(1)}) custom-call(s32[6]{0:T(128)S(1)} %stack.27.place, bf16[16,128,256]{2,1,0:T(8,128)(2,1)} %collective-permute-done.18.own, bf16[16,128,256]{2,1,0:T(8,128)(2,1)} %collective-permute-done.19.one, ...), custom_call_target="tpu_custom_call" | custom-call | tf_op jit(solution)/shard_map/pallas_call | solution.py:89
  65.4 4.5 %shard_map.149 = (bf16[128,4096]{1,0:T(8,128)(2,1)S(1)}, bf16[128,4096]{1,0:T(8,128)(2,1)S(1)}) custom-call(s32[6]{0:T(128)S(1)} %stack.27.place, bf16[128,1536]{1,0:T(8,128)(2,1)S(1)} %get-tuple-element.46.picked, bf16[128,1536]{1,0:T(8,128)(2,1)S(1)} %copy-done.7, bf16[2,1536,256]{2,1,0:T(8,128)(2,1)S(1)} %get-tuple-element.42.m1, ...), custom_call_target="tpu_custom_call" | custom-call | tf_op jit(solution)/shard_map/pallas_call | solution.py:89
  70.5 2.7 %collective-permute-done.24.picked_other = bf16[128,1536]{1,0:T(8,128)(2,1)S(1)} collective-permute-done((bf16[128,1536]{1,0:T(8,128)(2,1)S(1)}, bf16[128,1536]{1,0:T(8,128)(2,1)S(1)}, u32[]{:S(2)}, u32[]{:S(2)}) %collective-permute-start.24) | collective-permute-done | bytes 393248 | tf_op jit(solution)/shard_map/ppermute | solution.py:63
  73.2 2.1 shard_map.150
  76.1 2.9 %collective-permute-start.36 = (bf16[16,128,256]{2,1,0:T(8,128)(2,1)S(1)}, bf16[16,128,256]{2,1,0:T(8,128)(2,1)S(1)}, u32[]{:S(2)}, u32[]{:S(2)}) collective-permute-start(bf16[16,128,256]{2,1,0:T(8,128)(2,1)S(1)} %get-tuple-element.54), channel_id=1, source_target_pairs={{0,3},{1,0},{2,1},{3,2},{8,11},{9,8},{10,9},{11,10},{16,19},{17,16... | collective-permute-start | bytes 3145736 | tf_op jit(solution)/shard_map/ppermute | solution.py:59
  79.0 1.4 collective-permute-start.37
  80.4 11.3 %collective-permute-done.35.b = bf16[16,128,256]{2,1,0:T(8,128)(2,1)S(1)} collective-permute-done((bf16[16,128,256]{2,1,0:T(8,128)(2,1)S(1)}, bf16[16,128,256]{2,1,0:T(8,128)(2,1)S(1)}, u32[]{:S(2)}, u32[]{:S(2)}) %collective-permute-start.35) | collective-permute-done | bytes 1048608 | tf_op jit(solution)/shard_map/ppermute | solution.py:59
  91.7 10.9 %collective-permute-done.36.c = bf16[16,128,256]{2,1,0:T(8,128)(2,1)S(1)} collective-permute-done((bf16[16,128,256]{2,1,0:T(8,128)(2,1)S(1)}, bf16[16,128,256]{2,1,0:T(8,128)(2,1)S(1)}, u32[]{:S(2)}, u32[]{:S(2)}) %collective-permute-start.36) | collective-permute-done | bytes 1048608 | tf_op jit(solution)/shard_map/ppermute | solution.py:59
  102.5 1.8 collective-permute-done.37.d
  105.5 19.9 %all_to_all.16.pieces = bf16[16,128,256]{2,1,0:T(8,128)(2,1)S(1)} all-to-all(bf16[16,128,256]{2,1,0:T(8,128)(2,1)S(1)} %shard_map.151), channel_id=1, replica_groups={{0,4,64,68,8,12,72,76,16,20,80,84,24,28,88,92},{1,5,65,69,9,13,73,77,17..., dimensions={0} | all-to-all | bytes 2097152 | tf_op jit(solution)/shard_map/all_to_all | solution.py:54
  125.4 1.8 shard_map.152
  127.3 3.7 %all-to-all-start.2 = ((bf16[16,128,256]{2,1,0:T(8,128)(2,1)}), bf16[16,128,256]{2,1,0:T(8,128)(2,1)S(1)}, u32[]{:S(2)}, u32[]{:S(2)}) async-start(bf16[16,128,256]{2,1,0:T(8,128)(2,1)} %get-tuple-element.59), calls=%async_computation.2 | async-start | bytes 2097152 | tf_op jit(solution)/shard_map/all_to_all | solution.py:54
  133.3 3.3 %collective-permute-start.3 = (f32[8,128]{1,0:T(8,128)S(1)}, f32[8,128]{1,0:T(8,128)S(1)}, u32[]{:S(2)}, u32[]{:S(2)}) collective-permute-start(f32[8,128]{1,0:T(8,128)S(1)} %max.60), channel_id=1, source_target_pairs={{0,64},{1,65},{2,66},{3,67},{8,72},{9,73},{10,74},{11,75},{16,80},... | collective-permute-start | bytes 12296 | tf_op jit(solution)/shard_map/ppermute | solution.py:59
  138.6 6.7 %collective-permute-done.3 = f32[8,128]{1,0:T(8,128)S(1)} collective-permute-done((f32[8,128]{1,0:T(8,128)S(1)}, f32[8,128]{1,0:T(8,128)S(1)}, u32[]{:S(2)}, u32[]{:S(2)}) %collective-permute-start.3) | collective-permute-done | bytes 4128 | tf_op jit(solution)/shard_map/ppermute | solution.py:59
  145.4 1.2 collective-permute-start.6
  146.6 2.2 collective-permute-start.5
  149.3 3.2 %collective-permute-start.15 = (bf16[3,3,16,128]{3,2,1,0:T(8,128)(2,1)S(1)}, bf16[3,3,16,128]{3,2,1,0:T(8,128)(2,1)S(1)}, u32[]{:S(2)}, u32[]{:S(2)}) collective-permute-start(bf16[3,3,16,128]{3,2,1,0:T(8,128)(2,1)S(1)} %get-tuple-element.81), channel_id=1, source_target_pairs={{32,0},{64,32},{96,64},{0,96},{33,1},{65,33},{97,65},{1,97},{34,2}... | collective-permute-start | bytes 110600 | tf_op jit(solution)/shard_map/ppermute | solution.py:357
  153.6 2.6 %collective-permute-start.9 = (f32[8,128]{1,0:T(8,128)S(1)}, f32[8,128]{1,0:T(8,128)S(1)}, u32[]{:S(2)}, u32[]{:S(2)}) collective-permute-start(f32[8,128]{1,0:T(8,128)S(1)} %maximum_maximum_fusion.4), channel_id=1, source_target_pairs={{0,2},{1,3},{2,0},{3,1},{8,10},{9,11},{10,8},{11,9},{16,18},{17,19... | collective-permute-start | bytes 12296 | tf_op jit(solution)/shard_map/ppermute | solution.py:59
  156.2 1.5 collective-permute-start.8
  158.7 1.5 collective-permute-start.16
  160.2 4.8 %collective-permute-start.17 = (bf16[3,16,3,128]{3,2,1,0:T(4,128)(2,1)S(1)}, bf16[3,16,3,128]{3,2,1,0:T(4,128)(2,1)S(1)}, u32[]{:S(2)}, u32[]{:S(2)}) collective-permute-start(bf16[3,16,3,128]{3,2,1,0:T(4,128)(2,1)S(1)} %get-tuple-element.79), channel_id=1, source_target_pairs={{1,0},{2,1},{3,2},{4,3},{5,4},{6,5},{7,6},{8,7},{9,8},{10,9},{11,1... | collective-permute-start | bytes 110600 | tf_op jit(solution)/shard_map/ppermute | solution.py:357
  165.0 3.2 %collective-permute-start.43 = (bf16[16,128,256]{2,1,0:T(8,128)(2,1)S(1)}, bf16[16,128,256]{2,1,0:T(8,128)(2,1)S(1)}, u32[]{:S(2)}, u32[]{:S(2)}) collective-permute-start(bf16[16,128,256]{2,1,0:T(8,128)(2,1)S(1)} %all-to-all-done.2.own), channel_id=1, source_target_pairs={{0,3},{1,0},{2,1},{3,2},{8,11},{9,8},{10,9},{11,10},{16,19},{17,16... | collective-permute-start | bytes 3145736 | tf_op jit(solution)/shard_map/ppermute | solution.py:150
  168.3 8.2 %shard_map.147 = (f32[3,16,16,128]{3,2,1,0:T(8,128)S(1)}, f32[8,128]{1,0:T(8,128)S(1)}) custom-call(f32[8,128]{1,0:T(8,128)S(1)} %maximum_maximum_fusion.3.tops, f32[3,16,16,128]{3,2,1,0:T(8,128)S(1)} %copy-done, f32[3,3,16,128]{3,2,1,0:T(8,128)S(1)} %convert_element_type.31.low_x, f32[3,3,16,128]{3,2,1,0:T(8,128)S(1)} %convert_element_type.32.high_x, ...), custom_call_target="tpu_custom_call" | custom-call | tf_op jit(solution)/shard_map/pallas_call | solution.py:436
  177.7 1.3 collective-permute-start.28
  179.5 1.6 collective-permute-start.26
  181.1 1.8 collective-permute-done.28
  182.9 1.4 collective-permute-done.26
  184.3 1.4 collective-permute-start.31
  185.7 2.4 %collective-permute-start.30 = (f32[8,128]{1,0:T(8,128)S(1)}, f32[8,128]{1,0:T(8,128)S(1)}, u32[]{:S(2)}, u32[]{:S(2)}) collective-permute-start(f32[8,128]{1,0:T(8,128)S(1)} %maximum_maximum_fusion.2), channel_id=1, source_target_pairs={{0,24},{1,25},{2,26},{3,27},{8,0},{9,1},{10,2},{11,3},{16,8},{17,9... | collective-permute-start | bytes 12296 | tf_op jit(solution)/shard_map/ppermute | solution.py:59
  188.1 1.3 collective-permute-done.31
  189.4 3.5 %collective-permute-done.29 = f32[8,128]{1,0:T(8,128)S(1)} collective-permute-done((f32[8,128]{1,0:T(8,128)S(1)}, f32[8,128]{1,0:T(8,128)S(1)}, u32[]{:S(2)}, u32[]{:S(2)}) %collective-permute-start.29) | collective-permute-done | bytes 4128 | tf_op jit(solution)/shard_map/ppermute | solution.py:59
  192.9 3.5 %collective-permute-start.33 = (f32[8,128]{1,0:T(8,128)S(1)}, f32[8,128]{1,0:T(8,128)S(1)}, u32[]{:S(2)}, u32[]{:S(2)}) collective-permute-start(f32[8,128]{1,0:T(8,128)S(1)} %maximum_maximum_fusion.1), channel_id=1, source_target_pairs={{0,3},{1,0},{2,1},{3,2},{8,11},{9,8},{10,9},{11,10},{16,19},{17,16... | collective-permute-start | bytes 12296 | tf_op jit(solution)/shard_map/ppermute | solution.py:59
  196.4 1.6 collective-permute-done.34
  198.0 1.7 collective-permute-start.39
  200.8 5.1 %collective-permute-start.41 = (bf16[3,16,3,128]{3,2,1,0:T(4,128)(2,1)S(1)}, bf16[3,16,3,128]{3,2,1,0:T(4,128)(2,1)S(1)}, u32[]{:S(2)}, u32[]{:S(2)}) collective-permute-start(bf16[3,16,3,128]{3,2,1,0:T(4,128)(2,1)S(1)} %get-tuple-element.75), channel_id=1, source_target_pairs={{1,0},{2,1},{3,2},{4,3},{5,4},{6,5},{7,6},{8,7},{9,8},{10,9},{11,1... | collective-permute-start | bytes 110600 | tf_op jit(solution)/shard_map/ppermute | solution.py:357
  206.0 4.7 %collective-permute-done.32 = f32[8,128]{1,0:T(8,128)S(1)} collective-permute-done((f32[8,128]{1,0:T(8,128)S(1)}, f32[8,128]{1,0:T(8,128)S(1)}, u32[]{:S(2)}, u32[]{:S(2)}) %collective-permute-start.32) | collective-permute-done | bytes 4128 | tf_op jit(solution)/shard_map/ppermute | solution.py:59
  211.5 3.1 %collective-permute-start.45 = (bf16[8,128,256]{2,1,0:T(8,128)(2,1)S(1)}, bf16[8,128,256]{2,1,0:T(8,128)(2,1)S(1)}, u32[]{:S(2)}, u32[]{:S(2)}) collective-permute-start(bf16[8,128,256]{2,1,0:T(8,128)(2,1)S(1)} %slice.59), channel_id=1, source_target_pairs={{0,3},{1,0},{2,1},{3,2},{8,11},{9,8},{10,9},{11,10},{16,19},{17,16... | collective-permute-start | bytes 1572872 | tf_op jit(solution)/shard_map/ppermute | solution.py:150
  214.5 6.6 %collective-permute-done.44.low = bf16[8,128,256]{2,1,0:T(8,128)(2,1)S(1)} collective-permute-done((bf16[8,128,256]{2,1,0:T(8,128)(2,1)S(1)}, bf16[8,128,256]{2,1,0:T(8,128)(2,1)S(1)}, u32[]{:S(2)}, u32[]{:S(2)}) %collective-permute-start.44) | collective-permute-done | bytes 524320 | tf_op jit(solution)/shard_map/ppermute | solution.py:150
  221.7 8.8 %shard_map.153 = (f32[3,16,16,128]{3,2,1,0:T(8,128)S(1)}, f32[8,128]{1,0:T(8,128)}) custom-call(f32[8,128]{1,0:T(8,128)S(1)} %maximum_maximum_fusion.tops, f32[3,16,16,128]{3,2,1,0:T(8,128)S(1)} %get-tuple-element.61.field, f32[3,3,16,128]{3,2,1,0:T(8,128)S(1)} %convert_element_type.36.low_x, f32[3,3,16,128]{3,2,1,0:T(8,128)S(1)} %convert_element_type.37.high_x, ...), custom_call_target="tpu_custom_call" | custom-call | tf_op jit(solution)/shard_map/pallas_call | solution.py:436
  232.7 4.1 %shard_map.156 = f32[3,16,16,128]{3,2,1,0:T(8,128)} custom-call(s32[6]{0:T(128)S(1)} %stack.27.place, bf16[64,1536]{1,0:T(8,128)(2,1)S(1)} %copy-done.12, f32[3,16,16,128]{3,2,1,0:T(8,128)S(1)} %get-tuple-element.62.field, bf16[2,1536,256]{2,1,0:T(8,128)(2,1)S(1)} %get-tuple-element.63.m1, bf16[2,1024,256]{2,1,0:T(8,128)(2,1)S(1)} %get-tuple-element.64.m2, ...), custom_call_target="tpu_custom_call" | custom-call | tf_op jit(solution)/shard_map/pallas_call | solution.py:89
  (130 shorter events, 23.0 us)
Async XLA Ops:
  29.4 16.0 %collective-permute-start.10 = (bf16[16,128,256]{2,1,0:T(8,128)(2,1)S(1)}, bf16[16,128,256]{2,1,0:T(8,128)(2,1)S(1)}, u32[]{:S(2)}, u32[]{:S(2)}) collective-permute-start(bf16[16,128,256]{2,1,0:T(8,128)(2,1)S(1)} %all_to_all.15.own), channel_id=1, source_target_pairs={{0,1},{1,2},{2,3},{3,0},{8,9},{9,10},{10,11},{11,8},{16,17},{17,18... | collective-permute-start | bytes 3145736 | tf_op jit(solution)/shard_map/ppermute | solution.py:150
  30.9 14.9 %collective-permute-start.11 = (bf16[16,128,256]{2,1,0:T(8,128)(2,1)S(1)}, bf16[16,128,256]{2,1,0:T(8,128)(2,1)S(1)}, u32[]{:S(2)}, u32[]{:S(2)}) collective-permute-start(bf16[16,128,256]{2,1,0:T(8,128)(2,1)S(1)} %all_to_all.15.own), channel_id=1, source_target_pairs={{0,3},{1,0},{2,1},{3,2},{8,11},{9,8},{10,9},{11,10},{16,19},{17,16... | collective-permute-start | bytes 3145736 | tf_op jit(solution)/shard_map/ppermute | solution.py:150
  32.7 30.0 %collective-permute-start.18 = (bf16[16,128,256]{2,1,0:T(8,128)(2,1)S(1)}, bf16[16,128,256]{2,1,0:T(8,128)(2,1)}, u32[]{:S(2)}, u32[]{:S(2)}) collective-permute-start(bf16[16,128,256]{2,1,0:T(8,128)(2,1)S(1)} %all_to_all.15.own), channel_id=1, source_target_pairs={{0,32},{32,0},{1,33},{33,1},{2,34},{34,2},{3,35},{35,3},{4,36},{36... | collective-permute-start | bytes 3145736 | tf_op jit(solution)/shard_map/ppermute | solution.py:63
  45.5 10.6 %collective-permute-start.12 = (bf16[8,128,256]{2,1,0:T(8,128)(2,1)S(1)}, bf16[8,128,256]{2,1,0:T(8,128)(2,1)}, u32[]{:S(2)}, u32[]{:S(2)}) collective-permute-start(bf16[8,128,256]{2,1,0:T(8,128)(2,1)S(1)} %slice.48), channel_id=1, source_target_pairs={{0,1},{1,2},{2,3},{3,0},{8,9},{9,10},{10,11},{11,8},{16,17},{17,18... | collective-permute-start | bytes 1572872 | tf_op jit(solution)/shard_map/ppermute | solution.py:150
  45.8 16.9 %collective-permute-start.19 = (bf16[16,128,256]{2,1,0:T(8,128)(2,1)S(1)}, bf16[16,128,256]{2,1,0:T(8,128)(2,1)}, u32[]{:S(2)}, u32[]{:S(2)}) collective-permute-start(bf16[16,128,256]{2,1,0:T(8,128)(2,1)S(1)} %collective-permute-done.10.one), channel_id=1, source_target_pairs={{0,32},{32,0},{1,33},{33,1},{2,34},{34,2},{3,35},{35,3},{4,36},{36... | collective-permute-start | bytes 3145736 | tf_op jit(solution)/shard_map/ppermute | solution.py:63
  45.9 16.9 %collective-permute-start.20 = (bf16[16,128,256]{2,1,0:T(8,128)(2,1)S(1)}, bf16[16,128,256]{2,1,0:T(8,128)(2,1)}, u32[]{:S(2)}, u32[]{:S(2)}) collective-permute-start(bf16[16,128,256]{2,1,0:T(8,128)(2,1)S(1)} %collective-permute-done.11.three), channel_id=1, source_target_pairs={{0,32},{32,0},{1,33},{33,1},{2,34},{34,2},{3,35},{35,3},{4,36},{36... | collective-permute-start | bytes 3145736 | tf_op jit(solution)/shard_map/ppermute | solution.py:63
  46.4 9.7 %collective-permute-start.13 = (bf16[8,128,256]{2,1,0:T(8,128)(2,1)S(1)}, bf16[8,128,256]{2,1,0:T(8,128)(2,1)}, u32[]{:S(2)}, u32[]{:S(2)}) collective-permute-start(bf16[8,128,256]{2,1,0:T(8,128)(2,1)S(1)} %slice.49), channel_id=1, source_target_pairs={{0,3},{1,0},{2,1},{3,2},{8,11},{9,8},{10,9},{11,10},{16,19},{17,16... | collective-permute-start | bytes 1572872 | tf_op jit(solution)/shard_map/ppermute | solution.py:150
  56.1 6.7 %collective-permute-start.21 = (bf16[8,128,256]{2,1,0:T(8,128)(2,1)}, bf16[8,128,256]{2,1,0:T(8,128)(2,1)}, u32[]{:S(2)}, u32[]{:S(2)}) collective-permute-start(bf16[8,128,256]{2,1,0:T(8,128)(2,1)} %collective-permute-done.12.low), channel_id=1, source_target_pairs={{0,32},{32,0},{1,33},{33,1},{2,34},{34,2},{3,35},{35,3},{4,36},{36... | collective-permute-start | bytes 1572872 | tf_op jit(solution)/shard_map/ppermute | solution.py:63
  56.1 6.6 %collective-permute-start.22 = (bf16[8,128,256]{2,1,0:T(8,128)(2,1)}, bf16[8,128,256]{2,1,0:T(8,128)(2,1)}, u32[]{:S(2)}, u32[]{:S(2)}) collective-permute-start(bf16[8,128,256]{2,1,0:T(8,128)(2,1)} %collective-permute-done.13.high_part), channel_id=1, source_target_pairs={{0,32},{32,0},{1,33},{33,1},{2,34},{34,2},{3,35},{35,3},{4,36},{36... | collective-permute-start | bytes 1572872 | tf_op jit(solution)/shard_map/ppermute | solution.py:63
  75.3 16.4 %collective-permute-start.35 = (bf16[16,128,256]{2,1,0:T(8,128)(2,1)S(1)}, bf16[16,128,256]{2,1,0:T(8,128)(2,1)S(1)}, u32[]{:S(2)}, u32[]{:S(2)}) collective-permute-start(bf16[16,128,256]{2,1,0:T(8,128)(2,1)S(1)} %get-tuple-element.57), channel_id=1, source_target_pairs={{0,1},{1,2},{2,3},{3,0},{8,9},{9,10},{10,11},{11,8},{16,17},{17,18... | collective-permute-start | bytes 3145736 | tf_op jit(solution)/shard_map/ppermute | solution.py:59
  76.1 26.4 %collective-permute-start.36 = (bf16[16,128,256]{2,1,0:T(8,128)(2,1)S(1)}, bf16[16,128,256]{2,1,0:T(8,128)(2,1)S(1)}, u32[]{:S(2)}, u32[]{:S(2)}) collective-permute-start(bf16[16,128,256]{2,1,0:T(8,128)(2,1)S(1)} %get-tuple-element.54), channel_id=1, source_target_pairs={{0,3},{1,0},{2,1},{3,2},{8,11},{9,8},{10,9},{11,10},{16,19},{17,16... | collective-permute-start | bytes 3145736 | tf_op jit(solution)/shard_map/ppermute | solution.py:59
  79.0 25.4 %collective-permute-start.37 = (bf16[16,128,256]{2,1,0:T(8,128)(2,1)S(1)}, bf16[16,128,256]{2,1,0:T(8,128)(2,1)S(1)}, u32[]{:S(2)}, u32[]{:S(2)}) collective-permute-start(bf16[16,128,256]{2,1,0:T(8,128)(2,1)S(1)} %get-tuple-element.58), channel_id=1, source_target_pairs={{0,2},{1,3},{2,0},{3,1},{8,10},{9,11},{10,8},{11,9},{16,18},{17,19... | collective-permute-start | bytes 3145736 | tf_op jit(solution)/shard_map/ppermute | solution.py:59
  127.3 37.7 %all-to-all-start.2 = ((bf16[16,128,256]{2,1,0:T(8,128)(2,1)}), bf16[16,128,256]{2,1,0:T(8,128)(2,1)S(1)}, u32[]{:S(2)}, u32[]{:S(2)}) async-start(bf16[16,128,256]{2,1,0:T(8,128)(2,1)} %get-tuple-element.59), calls=%async_computation.2 | async-start | bytes 2097152 | tf_op jit(solution)/shard_map/all_to_all | solution.py:54
  133.3 12.1 %collective-permute-start.3 = (f32[8,128]{1,0:T(8,128)S(1)}, f32[8,128]{1,0:T(8,128)S(1)}, u32[]{:S(2)}, u32[]{:S(2)}) collective-permute-start(f32[8,128]{1,0:T(8,128)S(1)} %max.60), channel_id=1, source_target_pairs={{0,64},{1,65},{2,66},{3,67},{8,72},{9,73},{10,74},{11,75},{16,80},... | collective-permute-start | bytes 12296 | tf_op jit(solution)/shard_map/ppermute | solution.py:59
  136.6 8.8 %collective-permute-start.2 = (f32[8,128]{1,0:T(8,128)S(1)}, f32[8,128]{1,0:T(8,128)S(1)}, u32[]{:S(2)}, u32[]{:S(2)}) collective-permute-start(f32[8,128]{1,0:T(8,128)S(1)} %max.60), channel_id=1, source_target_pairs={{0,68},{1,69},{2,70},{3,71},{8,76},{9,77},{10,78},{11,79},{16,84},... | collective-permute-start | bytes 12296 | tf_op jit(solution)/shard_map/ppermute | solution.py:59
  137.8 7.6 %collective-permute-start.1 = (f32[8,128]{1,0:T(8,128)S(1)}, f32[8,128]{1,0:T(8,128)S(1)}, u32[]{:S(2)}, u32[]{:S(2)}) collective-permute-start(f32[8,128]{1,0:T(8,128)S(1)} %max.60), channel_id=1, source_target_pairs={{0,4},{1,5},{2,6},{3,7},{8,12},{9,13},{10,14},{11,15},{16,20},{17,... | collective-permute-start | bytes 12296 | tf_op jit(solution)/shard_map/ppermute | solution.py:59
  145.4 7.1 %collective-permute-start.6 = (f32[8,128]{1,0:T(8,128)S(1)}, f32[8,128]{1,0:T(8,128)S(1)}, u32[]{:S(2)}, u32[]{:S(2)}) collective-permute-start(f32[8,128]{1,0:T(8,128)S(1)} %maximum_maximum_fusion.5), channel_id=1, source_target_pairs={{0,16},{1,17},{2,18},{3,19},{8,24},{9,25},{10,26},{11,27},{16,0},{... | collective-permute-start | bytes 12296 | tf_op jit(solution)/shard_map/ppermute | solution.py:59
  146.6 5.9 %collective-permute-start.5 = (f32[8,128]{1,0:T(8,128)S(1)}, f32[8,128]{1,0:T(8,128)S(1)}, u32[]{:S(2)}, u32[]{:S(2)}) collective-permute-start(f32[8,128]{1,0:T(8,128)S(1)} %maximum_maximum_fusion.5), channel_id=1, source_target_pairs={{0,24},{1,25},{2,26},{3,27},{8,0},{9,1},{10,2},{11,3},{16,8},{17,9... | collective-permute-start | bytes 12296 | tf_op jit(solution)/shard_map/ppermute | solution.py:59
  148.8 4.8 %collective-permute-start.4 = (f32[8,128]{1,0:T(8,128)S(1)}, f32[8,128]{1,0:T(8,128)S(1)}, u32[]{:S(2)}, u32[]{:S(2)}) collective-permute-start(f32[8,128]{1,0:T(8,128)S(1)} %maximum_maximum_fusion.5), channel_id=1, source_target_pairs={{0,8},{1,9},{2,10},{3,11},{8,16},{9,17},{10,18},{11,19},{16,24},{1... | collective-permute-start | bytes 12296 | tf_op jit(solution)/shard_map/ppermute | solution.py:59
  149.3 15.7 %collective-permute-start.14 = (bf16[3,3,16,128]{3,2,1,0:T(8,128)(2,1)S(1)}, bf16[3,3,16,128]{3,2,1,0:T(8,128)(2,1)S(1)}, u32[]{:S(2)}, u32[]{:S(2)}) collective-permute-start(bf16[3,3,16,128]{3,2,1,0:T(8,128)(2,1)S(1)} %get-tuple-element.82), channel_id=1, source_target_pairs={{0,32},{32,64},{64,96},{96,0},{1,33},{33,65},{65,97},{97,1},{2,34}... | collective-permute-start | bytes 110600 | tf_op jit(solution)/shard_map/ppermute | solution.py:356
  149.3 18.9 %collective-permute-start.15 = (bf16[3,3,16,128]{3,2,1,0:T(8,128)(2,1)S(1)}, bf16[3,3,16,128]{3,2,1,0:T(8,128)(2,1)S(1)}, u32[]{:S(2)}, u32[]{:S(2)}) collective-permute-start(bf16[3,3,16,128]{3,2,1,0:T(8,128)(2,1)S(1)} %get-tuple-element.81), channel_id=1, source_target_pairs={{32,0},{64,32},{96,64},{0,96},{33,1},{65,33},{97,65},{1,97},{34,2}... | collective-permute-start | bytes 110600 | tf_op jit(solution)/shard_map/ppermute | solution.py:357
  153.6 5.1 %collective-permute-start.9 = (f32[8,128]{1,0:T(8,128)S(1)}, f32[8,128]{1,0:T(8,128)S(1)}, u32[]{:S(2)}, u32[]{:S(2)}) collective-permute-start(f32[8,128]{1,0:T(8,128)S(1)} %maximum_maximum_fusion.4), channel_id=1, source_target_pairs={{0,2},{1,3},{2,0},{3,1},{8,10},{9,11},{10,8},{11,9},{16,18},{17,19... | collective-permute-start | bytes 12296 | tf_op jit(solution)/shard_map/ppermute | solution.py:59
  156.2 4.0 %collective-permute-start.8 = (f32[8,128]{1,0:T(8,128)S(1)}, f32[8,128]{1,0:T(8,128)S(1)}, u32[]{:S(2)}, u32[]{:S(2)}) collective-permute-start(f32[8,128]{1,0:T(8,128)S(1)} %maximum_maximum_fusion.4), channel_id=1, source_target_pairs={{0,3},{1,0},{2,1},{3,2},{8,11},{9,8},{10,9},{11,10},{16,19},{17,16... | collective-permute-start | bytes 12296 | tf_op jit(solution)/shard_map/ppermute | solution.py:59
  157.8 7.2 %collective-permute-start.7 = (f32[8,128]{1,0:T(8,128)S(1)}, f32[8,128]{1,0:T(8,128)S(1)}, u32[]{:S(2)}, u32[]{:S(2)}) collective-permute-start(f32[8,128]{1,0:T(8,128)S(1)} %maximum_maximum_fusion.4), channel_id=1, source_target_pairs={{0,1},{1,2},{2,3},{3,0},{8,9},{9,10},{10,11},{11,8},{16,17},{17,18... | collective-permute-start | bytes 12296 | tf_op jit(solution)/shard_map/ppermute | solution.py:59
  158.7 9.5 %collective-permute-start.16 = (bf16[3,16,3,128]{3,2,1,0:T(4,128)(2,1)S(1)}, bf16[3,16,3,128]{3,2,1,0:T(4,128)(2,1)S(1)}, u32[]{:S(2)}, u32[]{:S(2)}) collective-permute-start(bf16[3,16,3,128]{3,2,1,0:T(4,128)(2,1)S(1)} %get-tuple-element.80), channel_id=1, source_target_pairs={{0,1},{1,2},{2,3},{3,4},{4,5},{5,6},{6,7},{7,8},{8,9},{9,10},{10,1... | collective-permute-start | bytes 110600 | tf_op jit(solution)/shard_map/ppermute | solution.py:356
  160.2 8.1 %collective-permute-start.17 = (bf16[3,16,3,128]{3,2,1,0:T(4,128)(2,1)S(1)}, bf16[3,16,3,128]{3,2,1,0:T(4,128)(2,1)S(1)}, u32[]{:S(2)}, u32[]{:S(2)}) collective-permute-start(bf16[3,16,3,128]{3,2,1,0:T(4,128)(2,1)S(1)} %get-tuple-element.79), channel_id=1, source_target_pairs={{1,0},{2,1},{3,2},{4,3},{5,4},{6,5},{7,6},{8,7},{9,8},{10,9},{11,1... | collective-permute-start | bytes 110600 | tf_op jit(solution)/shard_map/ppermute | solution.py:357
  165.0 35.8 %collective-permute-start.42 = (bf16[16,128,256]{2,1,0:T(8,128)(2,1)S(1)}, bf16[16,128,256]{2,1,0:T(8,128)(2,1)S(1)}, u32[]{:S(2)}, u32[]{:S(2)}) collective-permute-start(bf16[16,128,256]{2,1,0:T(8,128)(2,1)S(1)} %all-to-all-done.2.own), channel_id=1, source_target_pairs={{0,1},{1,2},{2,3},{3,0},{8,9},{9,10},{10,11},{11,8},{16,17},{17,18... | collective-permute-start | bytes 3145736 | tf_op jit(solution)/shard_map/ppermute | solution.py:150
  165.0 40.9 %collective-permute-start.43 = (bf16[16,128,256]{2,1,0:T(8,128)(2,1)S(1)}, bf16[16,128,256]{2,1,0:T(8,128)(2,1)S(1)}, u32[]{:S(2)}, u32[]{:S(2)}) collective-permute-start(bf16[16,128,256]{2,1,0:T(8,128)(2,1)S(1)} %all-to-all-done.2.own), channel_id=1, source_target_pairs={{0,3},{1,0},{2,1},{3,2},{8,11},{9,8},{10,9},{11,10},{16,19},{17,16... | collective-permute-start | bytes 3145736 | tf_op jit(solution)/shard_map/ppermute | solution.py:150
  177.7 5.1 %collective-permute-start.28 = (f32[8,128]{1,0:T(8,128)S(1)}, f32[8,128]{1,0:T(8,128)S(1)}, u32[]{:S(2)}, u32[]{:S(2)}) collective-permute-start(f32[8,128]{1,0:T(8,128)S(1)} %max.70), channel_id=1, source_target_pairs={{0,64},{1,65},{2,66},{3,67},{8,72},{9,73},{10,74},{11,75},{16,80},... | collective-permute-start | bytes 12296 | tf_op jit(solution)/shard_map/ppermute | solution.py:59
  179.0 3.8 %collective-permute-start.27 = (f32[8,128]{1,0:T(8,128)S(1)}, f32[8,128]{1,0:T(8,128)S(1)}, u32[]{:S(2)}, u32[]{:S(2)}) collective-permute-start(f32[8,128]{1,0:T(8,128)S(1)} %max.70), channel_id=1, source_target_pairs={{0,68},{1,69},{2,70},{3,71},{8,76},{9,77},{10,78},{11,79},{16,84},... | collective-permute-start | bytes 12296 | tf_op jit(solution)/shard_map/ppermute | solution.py:59
  179.5 4.8 %collective-permute-start.26 = (f32[8,128]{1,0:T(8,128)S(1)}, f32[8,128]{1,0:T(8,128)S(1)}, u32[]{:S(2)}, u32[]{:S(2)}) collective-permute-start(f32[8,128]{1,0:T(8,128)S(1)} %max.70), channel_id=1, source_target_pairs={{0,4},{1,5},{2,6},{3,7},{8,12},{9,13},{10,14},{11,15},{16,20},{17,... | collective-permute-start | bytes 12296 | tf_op jit(solution)/shard_map/ppermute | solution.py:59
  184.3 5.1 %collective-permute-start.31 = (f32[8,128]{1,0:T(8,128)S(1)}, f32[8,128]{1,0:T(8,128)S(1)}, u32[]{:S(2)}, u32[]{:S(2)}) collective-permute-start(f32[8,128]{1,0:T(8,128)S(1)} %maximum_maximum_fusion.2), channel_id=1, source_target_pairs={{0,16},{1,17},{2,18},{3,19},{8,24},{9,25},{10,26},{11,27},{16,0},{... | collective-permute-start | bytes 12296 | tf_op jit(solution)/shard_map/ppermute | solution.py:59
  185.7 3.7 %collective-permute-start.30 = (f32[8,128]{1,0:T(8,128)S(1)}, f32[8,128]{1,0:T(8,128)S(1)}, u32[]{:S(2)}, u32[]{:S(2)}) collective-permute-start(f32[8,128]{1,0:T(8,128)S(1)} %maximum_maximum_fusion.2), channel_id=1, source_target_pairs={{0,24},{1,25},{2,26},{3,27},{8,0},{9,1},{10,2},{11,3},{16,8},{17,9... | collective-permute-start | bytes 12296 | tf_op jit(solution)/shard_map/ppermute | solution.py:59
  188.1 4.8 %collective-permute-start.29 = (f32[8,128]{1,0:T(8,128)S(1)}, f32[8,128]{1,0:T(8,128)S(1)}, u32[]{:S(2)}, u32[]{:S(2)}) collective-permute-start(f32[8,128]{1,0:T(8,128)S(1)} %maximum_maximum_fusion.2), channel_id=1, source_target_pairs={{0,8},{1,9},{2,10},{3,11},{8,16},{9,17},{10,18},{11,19},{16,24},{1... | collective-permute-start | bytes 12296 | tf_op jit(solution)/shard_map/ppermute | solution.py:59
  192.9 5.1 %collective-permute-start.34 = (f32[8,128]{1,0:T(8,128)S(1)}, f32[8,128]{1,0:T(8,128)S(1)}, u32[]{:S(2)}, u32[]{:S(2)}) collective-permute-start(f32[8,128]{1,0:T(8,128)S(1)} %maximum_maximum_fusion.1), channel_id=1, source_target_pairs={{0,2},{1,3},{2,0},{3,1},{8,10},{9,11},{10,8},{11,9},{16,18},{17,19... | collective-permute-start | bytes 12296 | tf_op jit(solution)/shard_map/ppermute | solution.py:59
  192.9 6.8 %collective-permute-start.33 = (f32[8,128]{1,0:T(8,128)S(1)}, f32[8,128]{1,0:T(8,128)S(1)}, u32[]{:S(2)}, u32[]{:S(2)}) collective-permute-start(f32[8,128]{1,0:T(8,128)S(1)} %maximum_maximum_fusion.1), channel_id=1, source_target_pairs={{0,3},{1,0},{2,1},{3,2},{8,11},{9,8},{10,9},{11,10},{16,19},{17,16... | collective-permute-start | bytes 12296 | tf_op jit(solution)/shard_map/ppermute | solution.py:59
  196.4 14.3 %collective-permute-start.38 = (bf16[3,3,16,128]{3,2,1,0:T(8,128)(2,1)S(1)}, bf16[3,3,16,128]{3,2,1,0:T(8,128)(2,1)S(1)}, u32[]{:S(2)}, u32[]{:S(2)}) collective-permute-start(bf16[3,3,16,128]{3,2,1,0:T(8,128)(2,1)S(1)} %get-tuple-element.78), channel_id=1, source_target_pairs={{0,32},{32,64},{64,96},{96,0},{1,33},{33,65},{65,97},{97,1},{2,34}... | collective-permute-start | bytes 110600 | tf_op jit(solution)/shard_map/ppermute | solution.py:356
  198.0 12.8 %collective-permute-start.39 = (bf16[3,3,16,128]{3,2,1,0:T(8,128)(2,1)S(1)}, bf16[3,3,16,128]{3,2,1,0:T(8,128)(2,1)S(1)}, u32[]{:S(2)}, u32[]{:S(2)}) collective-permute-start(bf16[3,3,16,128]{3,2,1,0:T(8,128)(2,1)S(1)} %get-tuple-element.77), channel_id=1, source_target_pairs={{32,0},{64,32},{96,64},{0,96},{33,1},{65,33},{97,65},{1,97},{34,2}... | collective-permute-start | bytes 110600 | tf_op jit(solution)/shard_map/ppermute | solution.py:357
  199.7 11.7 %collective-permute-start.40 = (bf16[3,16,3,128]{3,2,1,0:T(4,128)(2,1)S(1)}, bf16[3,16,3,128]{3,2,1,0:T(4,128)(2,1)S(1)}, u32[]{:S(2)}, u32[]{:S(2)}) collective-permute-start(bf16[3,16,3,128]{3,2,1,0:T(4,128)(2,1)S(1)} %get-tuple-element.76), channel_id=1, source_target_pairs={{0,1},{1,2},{2,3},{3,4},{4,5},{5,6},{6,7},{7,8},{8,9},{9,10},{10,1... | collective-permute-start | bytes 110600 | tf_op jit(solution)/shard_map/ppermute | solution.py:356
  200.8 10.7 %collective-permute-start.41 = (bf16[3,16,3,128]{3,2,1,0:T(4,128)(2,1)S(1)}, bf16[3,16,3,128]{3,2,1,0:T(4,128)(2,1)S(1)}, u32[]{:S(2)}, u32[]{:S(2)}) collective-permute-start(bf16[3,16,3,128]{3,2,1,0:T(4,128)(2,1)S(1)} %get-tuple-element.75), channel_id=1, source_target_pairs={{1,0},{2,1},{3,2},{4,3},{5,4},{6,5},{7,6},{8,7},{9,8},{10,9},{11,1... | collective-permute-start | bytes 110600 | tf_op jit(solution)/shard_map/ppermute | solution.py:357
  205.9 4.8 %collective-permute-start.32 = (f32[8,128]{1,0:T(8,128)S(1)}, f32[8,128]{1,0:T(8,128)S(1)}, u32[]{:S(2)}, u32[]{:S(2)}) collective-permute-start(f32[8,128]{1,0:T(8,128)S(1)} %maximum_maximum_fusion.1), channel_id=1, source_target_pairs={{0,1},{1,2},{2,3},{3,0},{8,9},{9,10},{10,11},{11,8},{16,17},{17,18... | collective-permute-start | bytes 12296 | tf_op jit(solution)/shard_map/ppermute | solution.py:59
  210.8 20.8 %collective-permute-start.46 = (bf16[16,128,256]{2,1,0:T(8,128)(2,1)S(1)}, bf16[16,128,256]{2,1,0:T(8,128)(2,1)S(1)}, u32[]{:S(2)}, u32[]{:S(2)}) collective-permute-start(bf16[16,128,256]{2,1,0:T(8,128)(2,1)S(1)} %all-to-all-done.2.own), channel_id=1, source_target_pairs={{0,32},{32,0},{1,33},{33,1},{2,34},{34,2},{3,35},{35,3},{4,36},{36... | collective-permute-start | bytes 3145736 | tf_op jit(solution)/shard_map/ppermute | solution.py:63
  210.8 10.4 %collective-permute-start.44 = (bf16[8,128,256]{2,1,0:T(8,128)(2,1)S(1)}, bf16[8,128,256]{2,1,0:T(8,128)(2,1)S(1)}, u32[]{:S(2)}, u32[]{:S(2)}) collective-permute-start(bf16[8,128,256]{2,1,0:T(8,128)(2,1)S(1)} %slice.58), channel_id=1, source_target_pairs={{0,1},{1,2},{2,3},{3,0},{8,9},{9,10},{10,11},{11,8},{16,17},{17,18... | collective-permute-start | bytes 1572872 | tf_op jit(solution)/shard_map/ppermute | solution.py:150
  210.8 20.8 %collective-permute-start.47 = (bf16[16,128,256]{2,1,0:T(8,128)(2,1)S(1)}, bf16[16,128,256]{2,1,0:T(8,128)(2,1)S(1)}, u32[]{:S(2)}, u32[]{:S(2)}) collective-permute-start(bf16[16,128,256]{2,1,0:T(8,128)(2,1)S(1)} %collective-permute-done.42.one), channel_id=1, source_target_pairs={{0,32},{32,0},{1,33},{33,1},{2,34},{34,2},{3,35},{35,3},{4,36},{36... | collective-permute-start | bytes 3145736 | tf_op jit(solution)/shard_map/ppermute | solution.py:63
  211.4 20.2 %collective-permute-start.48 = (bf16[16,128,256]{2,1,0:T(8,128)(2,1)S(1)}, bf16[16,128,256]{2,1,0:T(8,128)(2,1)S(1)}, u32[]{:S(2)}, u32[]{:S(2)}) collective-permute-start(bf16[16,128,256]{2,1,0:T(8,128)(2,1)S(1)} %collective-permute-done.43.three), channel_id=1, source_target_pairs={{0,32},{32,0},{1,33},{33,1},{2,34},{34,2},{3,35},{35,3},{4,36},{36... | collective-permute-start | bytes 3145736 | tf_op jit(solution)/shard_map/ppermute | solution.py:63
  211.5 9.8 %collective-permute-start.45 = (bf16[8,128,256]{2,1,0:T(8,128)(2,1)S(1)}, bf16[8,128,256]{2,1,0:T(8,128)(2,1)S(1)}, u32[]{:S(2)}, u32[]{:S(2)}) collective-permute-start(bf16[8,128,256]{2,1,0:T(8,128)(2,1)S(1)} %slice.59), channel_id=1, source_target_pairs={{0,3},{1,0},{2,1},{3,2},{8,11},{9,8},{10,9},{11,10},{16,19},{17,16... | collective-permute-start | bytes 1572872 | tf_op jit(solution)/shard_map/ppermute | solution.py:150
  221.2 10.4 %collective-permute-start.49 = (bf16[8,128,256]{2,1,0:T(8,128)(2,1)S(1)}, bf16[8,128,256]{2,1,0:T(8,128)(2,1)S(1)}, u32[]{:S(2)}, u32[]{:S(2)}) collective-permute-start(bf16[8,128,256]{2,1,0:T(8,128)(2,1)S(1)} %collective-permute-done.44.low), channel_id=1, source_target_pairs={{0,32},{32,0},{1,33},{33,1},{2,34},{34,2},{3,35},{35,3},{4,36},{36... | collective-permute-start | bytes 1572872 | tf_op jit(solution)/shard_map/ppermute | solution.py:63
  221.2 10.4 %collective-permute-start.50 = (bf16[8,128,256]{2,1,0:T(8,128)(2,1)S(1)}, bf16[8,128,256]{2,1,0:T(8,128)(2,1)S(1)}, u32[]{:S(2)}, u32[]{:S(2)}) collective-permute-start(bf16[8,128,256]{2,1,0:T(8,128)(2,1)S(1)} %collective-permute-done.45.high_part), channel_id=1, source_target_pairs={{0,32},{32,0},{1,33},{33,1},{2,34},{34,2},{3,35},{35,3},{4,36},{36... | collective-permute-start | bytes 1572872 | tf_op jit(solution)/shard_map/ppermute | solution.py:63
  (19 other events, 191.8 us)
